TPU v7x, 32 devices: a whole 2x2x4 slice. The times are simulated.
32 devices in a mesh: dp: 8 (over z, y), tensor: 4 (over x, core).
Axes of the slice: x: 2, y: 2, z: 4, core: 2. Of those that a mesh axis runs over, the one named last changes fastest.
Arguments:
- tokens: bfloat16 [2, 16384, 768], P(None, ('dp', 'tensor')), may hold values from -6 to 6
- segments: int32 [2, 16384], P(None, 'dp'), may hold values from 0 to 15, never falling along the last dimension, each value on 1 to 2000 neighbouring positions
- timesteps: int32 [2, 8], P(None, 'dp'), may hold values from 0 to 999
- cotangent: bfloat16 [2, 16384, 768], P(None, ('dp', 'tensor')), may hold values from -6 to 6
- w_qkv: bfloat16 [768, 2304], P('dp', 'tensor'), may hold values from -0.21875 to 0.21875
- w_out: bfloat16 [768, 768], P('tensor', 'dp'), may hold values from -2.5 to 2.5
- w_up: bfloat16 [768, 3072], P('dp', 'tensor'), may hold values from -0.21875 to 0.21875
- w_down: bfloat16 [3072, 768], P('tensor', 'dp'), may hold values from -0.109375 to 0.109375
- w_ada: bfloat16 [256, 4608], P(('dp', 'tensor')), may hold values from -0.375 to 0.375
- b_ada: bfloat16 [4608], P(('dp', 'tensor')), may hold values from -3 to 3
Outputs:
- output: bfloat16 [2, 16384, 768], P(None, ('dp', 'tensor'))
- d_tokens: float32 [2, 16384, 768], P(None, ('dp', 'tensor'))
- g_qkv: float32 [768, 2304], P('dp', 'tensor')
- g_out: float32 [768, 768], P('tensor', 'dp')
- g_up: float32 [768, 3072], P('dp', 'tensor')
- g_down: float32 [3072, 768], P('tensor', 'dp')
- g_ada: float32 [256, 4608], P(('dp', 'tensor'))
- g_bias: float32 [4608], P(('dp', 'tensor'))
Inputs may be any that keep to these rules, and one draw needn't show every extreme that they name: `segments`: along each micro-batch the numbers never fall; every document covers 1 to 2000 positions, one exactly 2000.
All inputs are finite; a program needn't handle non-finite values.
Results may differ from a plain program's by a relative error of at most 0.014.
The roundings to bfloat16 on the way count: a program that leaves them out, or rounds other values in their place, can miss the bound.
Values may be sent and summed in bfloat16 or wider, within the bound.
No kernel may reach another device: no remote copies, remote signals or barrier semaphores. Data moves between devices by JAX's collectives and lax.ppermute only.
A program may use at most 192 MiB of HBM per device.

v0:
```python
import functools
import math

import jax
import jax.numpy as jnp
from jax import lax
from jax.experimental import pallas as pl
from jax.experimental.pallas import tpu as pltpu
from jax.sharding import PartitionSpec as P

HEADS = 12
HD = 64
HALF = HD // 2
EPSILON = 1e-06
MASKED = -1e30
F32 = jnp.float32
BF16 = jnp.bfloat16
NN = (((1,), (0,)), ((), ()))
NT = (((1,), (1,)), ((), ()))
TN = (((0,), (0,)), ((), ()))
TT = (((0,), (1,)), ((), ()))


def dot(left, right, dims=NN):
    return lax.dot_general(left, right, dims, preferred_element_type=F32)


def pick(bit, zero, one):
    return jnp.where(bit == 0, zero, one)


def swap_far(value):
    return lax.ppermute(value, "tensor", [(i, i ^ 2) for i in range(4)])


def swap_near(value):
    return lax.ppermute(value, "tensor", [(i, i ^ 1) for i in range(4)])


def swap_dp(value, bit):
    count = lax.axis_size("dp")
    return lax.ppermute(value, "dp", [(i, i ^ (1 << bit)) for i in range(count)])


def after(value, other):
    return lax.optimization_barrier((value, other))[0]


def dp_bits():
    return lax.axis_size("dp").bit_length() - 1


def my_bit(bit):
    return (lax.axis_index("dp") >> bit) & 1


def gather_block(current, bit, done, arrival=lambda value: value):
    arrived = arrival(swap_dp(current, bit))
    place = sum(1 for other in done if other > bit)
    mine = my_bit(bit)
    return jnp.stack([pick(mine, current, arrived), pick(mine, arrived, current)], axis=place)


def halves(current, bit, left):
    place = left.index(bit)
    first = lax.index_in_dim(current, 0, place, keepdims=False)
    second = lax.index_in_dim(current, 1, place, keepdims=False)
    mine = my_bit(bit)
    return pick(mine, first, second), pick(mine, second, first).astype(BF16)


def by_bits(total):
    return total.reshape((2,) * dp_bits() + (-1, total.shape[-1]))


def gather_relative(value, first=lambda value, bit: value):
    current = value
    for bit in range(dp_bits()):
        current = first(current, bit)
        current = jnp.stack([current, swap_dp(current, bit)])
    return current.reshape((-1,) + value.shape)


def scatter_relative(terms, first=lambda value, bit: value):
    count = dp_bits()
    current = terms.reshape((2,) * count + terms.shape[1:])
    for bit in range(count):
        current = first(current, bit)
        place = count - 1 - bit
        kept = lax.index_in_dim(current, 0, place, keepdims=False)
        sent = lax.index_in_dim(current, 1, place, keepdims=False)
        current = kept + swap_dp(sent, bit)
    return current


def document_columns(row_ref, col_s):
    for start in range(0, row_ref.shape[1], 128):
        tile = jnp.broadcast_to(row_ref[0:1, start : start + 128], (128, 128))
        col_s[start : start + 128, :] = tile.T


def token_copies(refs, place, tok_s, sems):
    rows = tok_s.shape[0] // 4
    return [
        pltpu.make_async_copy(
            ref,
            tok_s.at[pl.ds(pl.multiple_of(jnp.bitwise_xor(place, r) * rows, rows), rows), :],
            sems.at[r],
        )
        for r, ref in enumerate(refs)
    ]


def same_documents(row_ref, col_s, rows, columns, size):
    return jnp.concatenate([col_s[rows, :]] * (size // 128), axis=1) == row_ref[0:1, columns]


def attend_kernel(
    m, bq, bk, heads, lo_ref, hi_ref, place_ref, t0, t1, t2, t3, mods_ref, wq_ref, cs_ref, sn_ref,
    row_ref, normed_hbm, qkv_ref, own_ref, far_ref, lse_ref,
    tok_s, normed_s, wq_s, key_s, acc_s, att_s, col_s, sem, token_sems,
):
    length, width = tok_s.shape
    rows = length // 4
    place = place_ref[0]
    copies = token_copies((t0, t1, t2, t3), place, tok_s, token_sems)
    for copy in copies:
        copy.start()
    wq_s[...] = wq_ref[...].T
    document_columns(row_ref, col_s)
    for copy in copies:
        copy.wait()
    shift = mods_ref[m : m + 1, 0:width]
    stretch = 1.0 + mods_ref[m : m + 1, width : 2 * width]
    step = min(256, rows)

    def project(i, _):
        piece = pl.ds(pl.multiple_of(i * step, step), step)
        unit, _ = normalize(tok_s[piece, :].astype(F32))
        normed = (unit * stretch + shift).astype(BF16)
        normed_s[piece, :] = normed
        packed = dot(wq_s[...], normed, NT)
        cosine = cs_ref[:, piece]
        sine = sn_ref[:, piece]
        for h in range(heads):
            base = 3 * HD * h

            def turned(row):
                a = packed[row : row + HALF]
                b = packed[row + HALF : row + HD]
                return jnp.concatenate([a * cosine - b * sine, a * sine + b * cosine], axis=0)

            qkv_ref[base : base + HD, piece] = turned(base).astype(BF16)
            keys = turned(base + HD)
            qkv_ref[base + HD : base + 2 * HD, piece] = keys.astype(BF16)
            key_s[h, piece, :] = keys.T.astype(BF16)
            qkv_ref[base + 2 * HD : base + 3 * HD, piece] = packed[
                base + 2 * HD : base + 3 * HD
            ].astype(BF16)
        return 0

    lax.fori_loop(0, length // step, project, 0)
    copy = pltpu.make_async_copy(normed_s, normed_hbm, sem)
    copy.start()

    def query_block(i, _):
        columns = pl.ds(pl.multiple_of(i * bq, bq), bq)
        queries = [
            qkv_ref[3 * HD * h : 3 * HD * h + HD, columns] * jnp.asarray(0.125, BF16)
            for h in range(heads)
        ]
        acc_s[...] = jnp.zeros_like(acc_s)

        def key_block(j, carry):
            keys = pl.ds(pl.multiple_of(j * bk, bk), bk)
            allowed = same_documents(row_ref, col_s, keys, columns, bq)
            scores = [dot(key_s[h, keys, :], queries[h]) for h in range(heads)]
            result, fades, lows = [], [], []
            for h in range(heads):
                top, total = carry[2 * h], carry[2 * h + 1]
                masked = jnp.where(allowed, scores[h], MASKED)
                new_top = jnp.maximum(top, jnp.max(masked, axis=0, keepdims=True))
                fade = jnp.exp(top - new_top)
                chances = jnp.exp(masked - new_top)
                total = fade * total + jnp.sum(chances, axis=0, keepdims=True)
                lows.append(chances.astype(BF16))
                fades.append(fade)
                result += [new_top, total]
            for h in range(heads):
                values = qkv_ref[3 * HD * h + 2 * HD : 3 * HD * h + 3 * HD, keys]
                acc_s[h] = acc_s[h] * fades[h] + dot(values, lows[h])
            return tuple(result)

        start = (jnp.full((1, bq), MASKED, F32), jnp.zeros((1, bq), F32)) * heads
        carry = lax.fori_loop(lo_ref[i], hi_ref[i], key_block, start)
        for h in range(heads):
            top, total = carry[2 * h], carry[2 * h + 1]
            att_s[HD * h : HD * h + HD, columns] = (acc_s[h] / total).astype(BF16)
            lse_ref[h, 0:1, columns] = top + jnp.log(total)
        return 0

    lax.fori_loop(0, length // bq, query_block, 0)
    half = length // 2
    mine = pl.multiple_of(place // 2 * half, half)
    away = pl.multiple_of(half - mine, half)
    own_ref[...] = att_s[:, pl.ds(mine, half)]
    far_ref[...] = att_s[:, pl.ds(away, half)]
    copy.wait()


def attend_back_kernel(
    bq, bk, heads, lo_ref, hi_ref, place_ref, qkv_ref, own_ref, far_ref, d_own_ref, d_far_ref,
    lse_ref, cs_ref, sn_ref, row_ref, wq_hbm, t0, t1, t2, t3,
    keep_ref, send_ref, back_s, sums_ref, q_s, k_s, v_s, g_s, dat_s, dq_s, dk_s, dv_s, inner_s,
    col_s, wq_s, tok_s, sems, token_sems,
):
    place = place_ref[0]
    copies = [
        pltpu.make_async_copy(wq_hbm, wq_s, sems),
        *token_copies((t0, t1, t2, t3), place, tok_s, token_sems),
    ]
    for copy in copies:
        copy.start()
    length = qkv_ref.shape[1]
    half = length // 2
    rows = length // 4
    document_columns(row_ref, col_s)
    mine = pl.multiple_of(place // 2 * half, half)
    away = pl.multiple_of(half - mine, half)
    for start, att_ref, d_ref in ((mine, own_ref, d_own_ref), (away, far_ref, d_far_ref)):
        piece = pl.ds(start, half)
        dat_s[:, piece] = d_ref[...]
        for h in range(heads):
            head = slice(HD * h, HD * h + HD)
            inner_s[h, 0:1, piece] = jnp.sum(
                att_ref[head, :].astype(F32) * d_ref[head, :].astype(F32), axis=0, keepdims=True
            )
            g_s[h, piece, :] = d_ref[head, :].T
    for h in range(heads):
        base = 3 * HD * h
        q_s[h] = qkv_ref[base : base + HD, :].T
        k_s[h] = qkv_ref[base + HD : base + 2 * HD, :].T
        v_s[h] = qkv_ref[base + 2 * HD : base + 3 * HD, :].T
    dq_s[...] = jnp.zeros_like(dq_s)

    def key_block(j, _):
        keys = pl.ds(pl.multiple_of(j * bk, bk), bk)
        dk_s[:, keys, :] = jnp.zeros((heads, bk, HD), F32)
        dv_s[:, keys, :] = jnp.zeros((heads, bk, HD), F32)

        def query_block(i, _):
            columns = pl.ds(pl.multiple_of(i * bq, bq), bq)
            allowed = same_documents(row_ref, col_s, keys, columns, bq)
            scores = [
                dot(
                    k_s[h, keys, :] * jnp.asarray(0.125, BF16),
                    qkv_ref[3 * HD * h : 3 * HD * h + HD, columns],
                )
                for h in range(heads)
            ]
            d_chances = [
                dot(v_s[h, keys, :], dat_s[HD * h : HD * h + HD, columns]) for h in range(heads)
            ]
            lows, d_lows = [], []
            for h in range(heads):
                chances = jnp.where(
                    allowed, jnp.exp(scores[h] - lse_ref[h, 0:1, columns]), 0.0
                )
                lows.append(chances.astype(BF16))
                d_lows.append((chances * (d_chances[h] - inner_s[h, 0:1, columns])).astype(BF16))
            for h in range(heads):
                base = 3 * HD * h
                dv_s[h, keys, :] += dot(lows[h], g_s[h, columns, :])
                dk_s[h, keys, :] += dot(d_lows[h], q_s[h, columns, :])
                dq_s[HD * h : HD * h + HD, columns] += dot(
                    qkv_ref[base + HD : base + 2 * HD, keys], d_lows[h]
                )
            return 0

        lax.fori_loop(lo_ref[j], hi_ref[j], query_block, 0)
        return 0

    lax.fori_loop(0, length // bk, key_block, 0)
    for copy in copies:
        copy.wait()
    step = min(256, rows)

    sums_ref[...] = jnp.zeros_like(sums_ref)
    for r, (ref, entry) in enumerate(
        ((keep_ref, 0), (send_ref, 0), (keep_ref, 1), (send_ref, 1))
    ):

        def finish(i, _):
            start = jnp.bitwise_xor(place, r) * rows + i * step
            piece = pl.ds(pl.multiple_of(start, step), step)
            cosine = cs_ref[:, piece] * 0.125
            sine = sn_ref[:, piece] * 0.125

            def turned_back(row, value):
                a = value[0:HALF, :]
                b = value[HALF:HD, :]
                back_s[row : row + HALF, piece] = (a * cosine + b * sine).astype(BF16)
                back_s[row + HALF : row + HD, piece] = (b * cosine - a * sine).astype(BF16)

            for h in range(heads):
                base = 3 * HD * h
                turned_back(base, dq_s[HD * h : HD * h + HD, piece])
                turned_back(base + HD, dk_s[h, piece, :].T)
                back_s[base + 2 * HD : base + 3 * HD, piece] = dv_s[h, piece, :].T.astype(BF16)
            part = dot(back_s[:, piece].T, wq_s[...], NT)
            unit, _ = normalize(tok_s[piece, :].astype(F32))
            sums_ref[0:1, :] += jnp.sum(part, axis=0, keepdims=True)
            sums_ref[1:2, :] += jnp.sum(part * unit, axis=0, keepdims=True)
            ref[entry, pl.ds(pl.multiple_of(i * step, step), step), :] = part.astype(ref.dtype)
            return 0

        lax.fori_loop(0, rows // step, finish, 0)

def project_grad_kernel(add, normed_ref, back_ref, *rest):
    if add:
        before_ref, *rest = rest
    out_ref, total_s = rest
    step = pl.program_id(0)

    @pl.when(step == 0)
    def _():
        total_s[...] = jnp.zeros_like(total_s)

    total_s[...] += dot(back_ref[...], normed_ref[...])

    @pl.when(step == pl.num_programs(0) - 1)
    def _():
        total = total_s[...].T
        out_ref[...] = total + before_ref[...] if add else total


def project_grad(normed, back, before):
    length, width = normed.shape
    size = back.shape[0]
    add = before is not None
    step = length // 4
    block = pl.BlockSpec((width, size), lambda i: (0, 0))
    return pl.pallas_call(
        functools.partial(project_grad_kernel, add),
        grid=(4,),
        in_specs=[
            pl.BlockSpec((step, width), lambda i: (i, 0)),
            pl.BlockSpec((size, step), lambda i: (0, i)),
        ]
        + [block] * add,
        out_specs=block,
        out_shape=jax.ShapeDtypeStruct((width, size), F32),
        scratch_shapes=[pltpu.VMEM((size, width), F32)],
        cost_estimate=pl.CostEstimate(
            flops=40 * length * width * size, bytes_accessed=length * width * 4, transcendentals=0
        ),
        name="project_grad",
    )(normed, back, *[before] * add)


def held(*shape):
    return pl.BlockSpec(shape, lambda i, *_: (0,) * len(shape), pipeline_mode=pl.Buffered(1))


ANYWHERE = pl.BlockSpec(memory_space=pl.ANY)


def attend(m, blocks, mods, wq, tables, doc_row, bounds, place, heads, bq, bk):
    rows, width = blocks[0].shape
    length = 4 * rows
    size = 3 * HD * heads
    return pl.pallas_call(
        functools.partial(attend_kernel, m, bq, bk, heads),
        grid_spec=pltpu.PrefetchScalarGridSpec(
            num_scalar_prefetch=3,
            grid=(1,),
            in_specs=[ANYWHERE] * 4
            + [
                held(*mods.shape),
                held(width, size),
                held(HALF, length),
                held(HALF, length),
                held(1, length),
            ],
            out_specs=[
                ANYWHERE,
                held(size, length),
                held(HD * heads, length // 2),
                held(HD * heads, length // 2),
                held(heads, 1, length),
            ],
            scratch_shapes=[
                pltpu.VMEM((length, width), BF16),
                pltpu.VMEM((length, width), BF16),
                pltpu.VMEM((size, width), BF16),
                pltpu.VMEM((heads, length, HD), BF16),
                pltpu.VMEM((heads, HD, bq), F32),
                pltpu.VMEM((HD * heads, length), BF16),
                pltpu.VMEM((length, 128), F32),
                pltpu.SemaphoreType.DMA(()),
                pltpu.SemaphoreType.DMA((4,)),
            ],
        ),
        out_shape=[
            jax.ShapeDtypeStruct((length, width), BF16),
            jax.ShapeDtypeStruct((size, length), BF16),
            jax.ShapeDtypeStruct((HD * heads, length // 2), BF16),
            jax.ShapeDtypeStruct((HD * heads, length // 2), BF16),
            jax.ShapeDtypeStruct((heads, 1, length), F32),
        ],
        cost_estimate=pl.CostEstimate(
            flops=heads * length * length * 2400,
            bytes_accessed=length * width * 8,
            transcendentals=heads * length * length // 2,
        ),
        compiler_params=pltpu.CompilerParams(vmem_limit_bytes=46 * 2**20),
        name="attend",
    )(*bounds, place, *blocks, mods, wq, *tables, doc_row)


def attend_back(
    blocks, qkv, att, d_att, lse, tables, doc_row, bounds, place, wq, heads, bq, bk
):
    size, length = qkv.shape
    width = wq.shape[0]
    rows = length // 4
    half = held(HD * heads, length // 2)
    return pl.pallas_call(
        functools.partial(attend_back_kernel, bq, bk, heads),
        grid_spec=pltpu.PrefetchScalarGridSpec(
            num_scalar_prefetch=3,
            grid=(1,),
            in_specs=[
                held(size, length),
                half,
                half,
                half,
                half,
                held(heads, 1, length),
                held(HALF, length),
                held(HALF, length),
                held(1, length),
            ]
            + [ANYWHERE] * 5,
            out_specs=[
                held(2, rows, width),
                held(2, rows, width),
                held(size, length),
                held(2, width),
            ],
            scratch_shapes=[pltpu.VMEM((heads, length, HD), BF16)] * 4
            + [
                pltpu.VMEM((heads * HD, length), BF16),
                pltpu.VMEM((heads * HD, length), F32),
                pltpu.VMEM((heads, length, HD), F32),
                pltpu.VMEM((heads, length, HD), F32),
                pltpu.VMEM((heads, 8, length), F32),
                pltpu.VMEM((length, 128), F32),
                pltpu.VMEM((width, size), BF16),
                pltpu.VMEM((length, width), BF16),
                pltpu.SemaphoreType.DMA(()),
                pltpu.SemaphoreType.DMA((4,)),
            ],
        ),
        out_shape=[
            jax.ShapeDtypeStruct((2, rows, width), F32),
            jax.ShapeDtypeStruct((2, rows, width), BF16),
            jax.ShapeDtypeStruct((size, length), BF16),
            jax.ShapeDtypeStruct((2, width), F32),
        ],
        cost_estimate=pl.CostEstimate(
            flops=heads * length * length * 3600,
            bytes_accessed=length * width * 8,
            transcendentals=heads * length * length // 2,
        ),
        compiler_params=pltpu.CompilerParams(vmem_limit_bytes=50 * 2**20),
        name="attend_back",
    )(*bounds, place, qkv, *att, *d_att, lse, *tables, doc_row, wq, *blocks)


def gelu_pair(values):
    square = values * values
    bend = jnp.tanh(0.7978845608028654 * (values + 0.044715 * (square * values)))
    slope = 0.7978845608028654 * (1.0 + 3 * 0.044715 * square)
    hidden = 0.5 * values * (1.0 + bend)
    return hidden, 0.5 * (1.0 + bend) + 0.5 * values * (1.0 - bend * bend) * slope


def feed_kernel(parts, add, n0, n1, g0, g1, up_ref, down_ref, *rest):
    if add:
        before_ref, *rest = rest
    b0, b1, d0, d1, g_ref, n_s, g_s, n_t, g_t, hidden_s, pre_s, b1_s, d1_s = rest
    rows = n0.shape[0]
    up = up_ref[...].reshape(-1, up_ref.shape[-1])
    down = down_ref[...].reshape(-1, down_ref.shape[-1])

    @pl.when(pl.program_id(0) == 0)
    def _():
        for piece, n, g in ((slice(0, rows), n0, g0), (slice(rows, 2 * rows), n1, g1)):
            n_s[piece, :] = n[...]
            g_s[piece, :] = g[...]
            n_t[:, piece] = n[...].T
            g_t[:, piece] = g[...].T
        for ref in (b0, b1_s, d0, d1_s):
            ref[...] = jnp.zeros_like(ref)

    step = 2 * rows // parts
    for p in range(parts):
        piece = slice(p * step, (p + 1) * step)
        hidden, slope = gelu_pair(dot(n_s[piece, :], up))
        hidden_s[piece, :] = hidden.astype(BF16)
        pre_s[piece, :] = (dot(g_s[piece, :], down) * slope).astype(BF16)
    for first, b_ref, d_ref in ((0, b0, d0), (rows, b1_s, d1_s)):
        for start in range(0, rows, step):
            piece = slice(first + start, first + start + step)
            b_ref[start : start + step, :] += dot(hidden_s[piece, :], down, NT)
            d_ref[start : start + step, :] += dot(pre_s[piece, :], up, NT)
    chunk = up.shape[1]
    for start, left, right in ((0, n_t, pre_s), (chunk, g_t, hidden_s)):
        columns = slice(start, start + chunk)
        grad = dot(left[...], right[...])
        if add:
            grad = grad + before_ref[:, columns]
        g_ref[:, columns] = grad.astype(g_ref.dtype)

    @pl.when(pl.program_id(0) == pl.num_programs(0) - 1)
    def _():
        b1[...] = b1_s[...].astype(BF16)
        d1[...] = d1_s[...].astype(BF16)


CHUNK = 256


def feed(normed, grads, pack, hid, before, kind):
    rows, width = normed[0].shape
    count, _, height, _ = pack.shape
    chunk = CHUNK
    steps = hid // chunk
    add = before is not None

    def weight(first):
        return pl.BlockSpec(
            (count, 1, height, chunk), lambda i: (0, i // steps, 0, first * steps + i % steps)
        )

    block = pl.BlockSpec((rows, width), lambda i: (0, 0))
    columns = pl.BlockSpec((width, 2 * chunk), lambda i: (0, i))
    total = 2 * rows
    return pl.pallas_call(
        functools.partial(feed_kernel, 4, add),
        grid=(2 * steps,),
        in_specs=[block] * 4 + [weight(0), weight(1)] + [columns] * add,
        out_specs=[block] * 4 + [columns],
        out_shape=[jax.ShapeDtypeStruct((rows, width), kind) for kind in (F32, BF16, F32, BF16)]
        + [jax.ShapeDtypeStruct((width, 4 * hid), kind)],
        scratch_shapes=[pltpu.VMEM((total, width), BF16)] * 2
        + [pltpu.VMEM((width, total), BF16)] * 2
        + [pltpu.VMEM((total, chunk), BF16)] * 2
        + [pltpu.VMEM((rows, width), F32)] * 2,
        cost_estimate=pl.CostEstimate(
            flops=24 * total * width * hid,
            bytes_accessed=8 * width * hid + 12 * total * width,
            transcendentals=2 * total * hid,
        ),
        compiler_params=pltpu.CompilerParams(vmem_limit_bytes=46 * 2**20),
        name="feed",
    )(*normed, *grads, pack, pack, *[before] * add)


def terms_kernel(cond_ref, w_ref, bias_ref, out_ref):
    total = bias_ref[...] + jnp.zeros_like(out_ref)
    for r in range(w_ref.shape[0]):
        total = total + cond_ref[:, r : r + 1] * w_ref[r : r + 1, :].astype(F32)
    out_ref[...] = total


def mod_terms(cond, w_ada, bias):
    return pl.pallas_call(
        terms_kernel,
        out_shape=jax.ShapeDtypeStruct((cond.shape[0], w_ada.shape[1]), F32),
        cost_estimate=pl.CostEstimate(
            flops=2 * cond.size * w_ada.shape[1],
            bytes_accessed=4 * cond.shape[0] * w_ada.shape[1],
            transcendentals=0,
        ),
        name="mod_terms",
    )(cond.astype(F32), w_ada, bias[None, :])


def part_of(mods_ref, m, k, width):
    return mods_ref[m : m + 1, k * width : (k + 1) * width]


def out_weights(pack_ref, side, size):
    return pack_ref[:, pl.ds(side, 1), :, 0:size].reshape(-1, size)


def out_kernel(place_ref, own_ref, far_ref, pack_ref, keep_ref, send_ref):
    size, total = own_ref.shape
    rows = total // 2
    side, near = place_ref[0] // 2, place_ref[0] % 2
    own_w = out_weights(pack_ref, side, size)
    far_w = out_weights(pack_ref, 1 - side, size)
    for ref, half in ((keep_ref, near), (send_ref, 1 - near)):
        piece = pl.ds(pl.multiple_of(half * rows, rows), rows)
        ref[...] = (
            dot(own_ref[:, piece].T, own_w, NT) + dot(far_ref[:, piece].T, far_w, NT)
        ).astype(ref.dtype)


def pack_tail(pack):
    count, _, height, columns = pack.shape
    return pl.BlockSpec((count, 2, height, CHUNK), lambda i, *_: (0, 0, 0, columns // CHUNK))


def out_project(place, own, away, pack):
    size, total = own.shape
    rows, width = total // 2, pack.shape[0] * pack.shape[2]
    return pl.pallas_call(
        out_kernel,
        grid_spec=pltpu.PrefetchScalarGridSpec(
            num_scalar_prefetch=1,
            grid=(1,),
            in_specs=[held(size, total), held(size, total), pack_tail(pack)],
            out_specs=[held(rows, width), held(rows, width)],
        ),
        out_shape=[
            jax.ShapeDtypeStruct((rows, width), F32),
            jax.ShapeDtypeStruct((rows, width), BF16),
        ],
        cost_estimate=pl.CostEstimate(
            flops=8 * total * width * size, bytes_accessed=total * width * 4, transcendentals=0
        ),
        compiler_params=pltpu.CompilerParams(vmem_limit_bytes=20 * 2**20),
        name="out_project",
    )(place, own, away, pack)


def out_back_kernel(add, place_ref, g0_ref, g1_ref, own_ref, far_ref, pack_ref, *rest):
    if add:
        *before_refs, = rest[:2]
        rest = rest[2:]
    d_own_ref, d_far_ref, *grad_refs = rest
    size, total = own_ref.shape
    rows = total // 2
    side, near = place_ref[0] // 2, place_ref[0] % 2
    pieces = [
        pl.ds(pl.multiple_of(half * rows, rows), rows) for half in (near, 1 - near)
    ]
    grads = [g0_ref[...], g1_ref[...]]
    turned = [grad.T for grad in grads]
    for k, (att_ref, d_ref, which) in enumerate(
        ((own_ref, d_own_ref, side), (far_ref, d_far_ref, 1 - side))
    ):
        weights = out_weights(pack_ref, which, size).T
        total_grad = 0.0
        for grad, flipped, piece in zip(grads, turned, pieces):
            d_ref[:, piece] = dot(weights, grad, NT).astype(BF16)
            total_grad = total_grad + dot(flipped, att_ref[:, piece], NT)
        if add:
            total_grad = total_grad + before_refs[k][...]
        grad_refs[k][...] = total_grad.astype(grad_refs[k].dtype)


def out_back(place, grads, own, away, pack, before, last):
    size, total = own.shape
    rows, width = grads[0].shape
    add = before is not None
    half = held(size, total)
    return pl.pallas_call(
        functools.partial(out_back_kernel, add),
        grid_spec=pltpu.PrefetchScalarGridSpec(
            num_scalar_prefetch=1,
            grid=(1,),
            in_specs=[held(rows, width)] * 2
            + [half, half, pack_tail(pack)]
            + [held(width, size)] * (2 * add),
            out_specs=[half, half, held(width, size), held(width, size)],
        ),
        out_shape=[jax.ShapeDtypeStruct((size, total), BF16)] * 2
        + [
            jax.ShapeDtypeStruct((width, size), F32),
            jax.ShapeDtypeStruct((width, size), BF16 if last else F32),
        ],
        cost_estimate=pl.CostEstimate(
            flops=16 * total * width * size, bytes_accessed=total * width * 4, transcendentals=0
        ),
        compiler_params=pltpu.CompilerParams(vmem_limit_bytes=24 * 2**20),
        name="out_back",
    )(place, *grads, own, away, pack, *(before if add else ()))


def before_feed_kernel(m, mods_ref, tok_ref, cot_ref, keep_ref, arr_ref, br_ref, n_ref, g_ref):
    width = keep_ref.shape[1]
    branch = keep_ref[...] + arr_ref[...].astype(F32)
    br_ref[...] = branch
    middle = tok_ref[0].astype(F32) + part_of(mods_ref, m, 2, width) * branch
    unit, _ = normalize(middle)
    n_ref[...] = (
        unit * (1.0 + part_of(mods_ref, m, 4, width)) + part_of(mods_ref, m, 3, width)
    ).astype(BF16)
    g_ref[...] = (cot_ref[0].astype(F32) * part_of(mods_ref, m, 5, width)).astype(BF16)


def after_feed_kernel(
    m, mods_ref, tok_ref, cot_ref, br_ref, b0_ref, b1_ref, d0_ref, d1_ref, *rest
):
    out_ref, d_ref, g_ref, sums_ref = rest[-4:]
    width = br_ref.shape[1]
    branch_a = br_ref[...]
    middle = tok_ref[0].astype(F32) + part_of(mods_ref, m, 2, width) * branch_a
    unit, root = normalize(middle)
    branch_m = b0_ref[...] + b1_ref[...].astype(F32)
    out_ref[0] = (middle + part_of(mods_ref, m, 5, width) * branch_m).astype(BF16)
    d_normed = d0_ref[...] + d1_ref[...].astype(F32)
    grad = cot_ref[0].astype(F32)
    d_middle = grad + normalize_back(d_normed, unit, root, part_of(mods_ref, m, 4, width))
    d_ref[...] = d_middle
    g_ref[...] = (d_middle * part_of(mods_ref, m, 2, width)).astype(BF16)

    @pl.when(pl.program_id(0) == 0)
    def _():
        sums_ref[...] = jnp.zeros_like(sums_ref)

    for k, term in enumerate((d_middle * branch_a, d_normed, d_normed * unit, grad * branch_m)):
        sums_ref[k : k + 1, :] += jnp.sum(term, axis=0, keepdims=True)


def finish_kernel(m, mods_ref, tok_ref, keep_ref, arr_ref, crossed_ref, d_ref, *rest):
    out_ref = rest[-1]
    width = d_ref.shape[1]
    unit, root = normalize(tok_ref[0].astype(F32))
    grad = keep_ref[0] + arr_ref[0].astype(F32) + crossed_ref[...].astype(F32)
    out_ref[0] = d_ref[...] + normalize_back(grad, unit, root, part_of(mods_ref, m, 1, width))


def by_rows(name, kernel, m, mods, inputs, outputs, before=None, sums=0, weight=40):
    rows, width = inputs[-1].shape
    step = min(256, rows)
    flat = pl.BlockSpec((step, width), lambda i: (i, 0))
    entry = pl.BlockSpec((1, step, width), lambda i: (m, i, 0))
    first = pl.BlockSpec((1, step, width), lambda i: (0, i, 0))
    in_specs = [pl.BlockSpec(mods.shape, lambda i: (0, 0))]
    for value, whole_set in inputs[:-1]:
        in_specs.append(flat if value.ndim == 2 else entry if whole_set else first)
    values = [value for value, _ in inputs[:-1]] + [inputs[-1]]
    in_specs.append(flat)
    extra = [] if before is None else [before]
    in_specs += [ANYWHERE] * len(extra)
    out_specs = [flat if len(shape.shape) == 2 else entry for shape in outputs]
    if sums:
        outputs = [*outputs, jax.ShapeDtypeStruct((sums, width), F32)]
        out_specs.append(pl.BlockSpec((sums, width), lambda i: (0, 0)))
    return pl.pallas_call(
        functools.partial(kernel, m),
        grid=(rows // step,),
        in_specs=in_specs,
        out_specs=out_specs,
        out_shape=outputs,
        input_output_aliases={1 + len(values): 0} if extra else {},
        cost_estimate=pl.CostEstimate(
            flops=weight * rows * width, bytes_accessed=32 * rows * width, transcendentals=rows
        ),
        compiler_params=pltpu.CompilerParams(vmem_limit_bytes=16 * 2**20),
        name=name,
    )(mods, *values, *extra)


def block_range(doc_ids, rows, columns):
    by_row = doc_ids.reshape(-1, rows)
    by_column = doc_ids.reshape(-1, columns)
    low = jnp.sum(by_column[:, -1][None, :] < by_row[:, 0][:, None], axis=1, dtype=jnp.int32)
    high = jnp.sum(by_column[:, 0][None, :] <= by_row[:, -1][:, None], axis=1, dtype=jnp.int32)
    return low, high


def turn_tables(length):
    freqs = jnp.exp(-math.log(10000.0) * jnp.arange(HALF, dtype=F32) / HALF)
    angles = freqs[:, None] * jnp.arange(length, dtype=F32)[None, :]
    return jnp.cos(angles), jnp.sin(angles)


def normalize(values):
    center = values - jnp.mean(values, axis=-1, keepdims=True)
    root = lax.rsqrt(jnp.mean(center * center, axis=-1, keepdims=True) + EPSILON)
    return center * root, root


def normalize_back(grad, unit, root, stretch):
    turned = grad * (1.0 + stretch)
    return root * (
        turned
        - jnp.mean(turned, axis=-1, keepdims=True)
        - unit * jnp.mean(turned * unit, axis=-1, keepdims=True)
    )


def per_device(tokens, segments, timesteps, cotangent, w_qkv, w_out, w_up, w_down, w_ada, b_ada):
    micro_count, rows, width = tokens.shape
    heads = HEADS // 4
    length = 4 * rows
    count = dp_bits()
    tensor = lax.axis_index("tensor")
    far, near = tensor // 2, tensor % 2
    device = lax.axis_index("dp") * 4 + tensor
    falling = list(range(count - 1, -1, -1))
    rising = list(range(count))

    fq, fk = min(512, length), min(512, length)
    rq, rk = min(512, length), min(256, length)
    doc_rows = segments.astype(F32)
    bounds = [
        (block_range(segments[m], fq, fk), block_range(segments[m], rk, rq))
        for m in range(micro_count)
    ]
    tables = turn_tables(length)
    pack = jnp.concatenate([w_up, w_down.T, w_out.T], axis=1)

    states = []

    def advance(value, step):
        while len(states) <= step:
            done = falling[: len(states)]
            states.append(
                gather_block(states[-1] if states else w_qkv, falling[len(done)], done)
            )
        return after(value, states[step])

    def with_stamps(value, bit):
        if bit == count - 1:
            return after(value, (tables, doc_rows, bounds, pack))
        return advance(value, bit - 1) if bit >= 1 else value

    ready = tokens[0]
    across = swap_far(ready)
    blocks = [(ready, swap_near(ready), across, swap_near(across))]

    feature_rows = w_ada.shape[0]
    half = feature_rows * lax.axis_size("dp") * 4 // 2
    stamps = gather_relative(timesteps[:, 0].astype(F32), with_stamps)
    index = device * feature_rows + jnp.arange(feature_rows)
    freqs = jnp.exp(-math.log(10000.0) * (index % half).astype(F32) / half)
    angles = stamps[:, :, None] * freqs
    cond = jnp.where(index < half, jnp.cos(angles), jnp.sin(angles)).astype(BF16)
    cond = cond.reshape(-1, feature_rows)
    bias_size = b_ada.shape[0]
    slots = w_ada.shape[1] // bias_size
    bias = jnp.where(
        jnp.arange(slots)[:, None] == device, b_ada.astype(F32)[None, :], 0.0
    ).reshape(-1)
    terms = mod_terms(advance(after(cond, across), count - 2), w_ada, bias)
    mods = scatter_relative(terms.reshape(-1, micro_count, terms.shape[1]))

    begun = mods
    mods = after(advance(mods, count - 1), blocks[0][3])
    wq = states[-1].reshape(width, -1)
    mods = mods + swap_far(mods)
    mods = mods + swap_near(mods)

    pack = after(pack, begun)
    groups = [
        [4 * i + 2 * j + c for i in range(lax.axis_size("dp")) for j in range(2)] for c in range(2)
    ]
    pack = lax.all_gather(pack, ("dp", "tensor"), axis_index_groups=groups)
    pack = pack.reshape((-1, 2) + pack.shape[1:])
    hid = w_up.shape[1]
    part = w_out.shape[0]
    if w_up.shape[0] % 16:
        pack = pack.transpose(1, 0, 2, 3).reshape(1, 2, width, -1)

    place = tensor.astype(jnp.int32).reshape(1)
    state = []
    for m in range(micro_count):
        if m > 0:
            own = after(tokens, mods)[m]
            across = after(swap_far(own), state[-1][3])
            blocks.append((own, swap_near(own), across, swap_near(across)))
        normed_a, qkv, att_own, att_away, lse = attend(
            m, blocks[m], mods, wq, tables, doc_rows[m : m + 1],
            bounds[m][0], place, heads, fq, fk,
        )
        state.append((normed_a, qkv, (att_own, att_away), lse))

    every = jax.ShapeDtypeStruct(tokens.shape, BF16)
    wide = jax.ShapeDtypeStruct((rows, width), F32)
    low = jax.ShapeDtypeStruct((rows, width), BF16)
    output = None
    grads_out = None
    grads_feed = None
    middles = []
    for m in range(micro_count):
        last = m + 1 == micro_count
        att_own, att_away = state[m][2]
        if m == 0:
            crossing = [swap_far(state[k][2][1]) for k in range(micro_count)]
        att_far = crossing[m]
        if not last:
            att_far = after(att_far, state[m + 1][2][0])
        keep, send = out_project(place, att_own, att_far, pack)
        branch_a, normed_m, grad_m = by_rows(
            "before_feed",
            before_feed_kernel,
            m,
            mods,
            [(tokens, True), (cotangent, True), (keep, False), swap_near(send)],
            [wide, low, low],
        )
        if m > 0:
            normed_m = after(normed_m, middles[-1][3])
        branch_own, branch_near, d_own, d_near, grads_feed = feed(
            (normed_m, swap_near(normed_m)),
            (grad_m, swap_near(grad_m)),
            pack,
            hid,
            grads_feed,
            BF16 if last else F32,
        )
        if not last:
            (branch_own, branch_near, d_own, d_near), crossing[m + 1] = lax.optimization_barrier(
                ((branch_own, branch_near, d_own, d_near), crossing[m + 1])
            )
        if m > 0:
            (branch_own, branch_near, d_own, d_near), middles[m - 1][1][1] = (
                lax.optimization_barrier(
                    ((branch_own, branch_near, d_own, d_near), middles[m - 1][1][1])
                )
            )
        output, d_middle, grad_a, sums = by_rows(
            "after_feed",
            after_feed_kernel,
            m,
            mods,
            [
                (tokens, True),
                (cotangent, True),
                (branch_a, False),
                (branch_own, False),
                (swap_near(branch_near), False),
                (d_own, False),
                swap_near(d_near),
            ],
            [every, wide, low],
            before=output,
            sums=4,
        )
        d_att_own, d_att_far, *grads_out = out_back(
            place, (grad_a, swap_near(grad_a)), att_own, att_far, pack, grads_out,
            last,
        )
        if m > 0:
            middles[m - 1][1][0] = after(middles[m - 1][1][0], d_att_far)
        middles.append([d_middle, [d_att_own, swap_far(d_att_far)], sums, d_att_far])

    feed_total = lax.psum_scatter(grads_feed, "dp", scatter_dimension=0, tiled=True)
    out_far = swap_far(grads_out[1])

    mod_grads = []
    g_qkv = None
    backs = []
    for m in range(micro_count):
        normed_a, qkv, att, lse = state[m]
        keep, send, back, sums = attend_back(
            blocks[m], qkv, att, middles[m][1], lse, tables, doc_rows[m : m + 1],
            bounds[m][1], place, wq, heads, rq, rk,
        )
        if m > 0:
            (keep, send, back, sums), (backs[m - 1][2], out_half) = lax.optimization_barrier(
                ((keep, send, back, sums), (backs[m - 1][2], out_half))
            )
        elif m == 0:
            (keep, send, back, sums), out_far = lax.optimization_barrier(
                ((keep, send, back, sums), out_far)
            )
            out_keep, out_send = halves(
                by_bits(grads_out[0] + out_far.astype(F32)), 0, falling
            )
            out_half = swap_dp(out_send, 0)
        arrived = swap_near(send)
        crossing = (keep[1] + arrived[1].astype(F32)).astype(BF16)
        crossed = swap_far(crossing)
        g_qkv = project_grad(normed_a, back, g_qkv)
        if m + 1 < micro_count:
            middles[m + 1][1][0] = after(
                middles[m + 1][1][0], (crossing, g_qkv, out_send)
            )
            middles[m + 1][1][1] = after(middles[m + 1][1][1], sums)
        backs.append([keep, arrived, crossed])
        mod_grads.append(jnp.concatenate([sums.reshape(-1), middles[m][2].reshape(-1)]))
    g_last = after(g_qkv, crossing)
    middles[0][0] = after(middles[0][0], g_last)
    d_tokens = None
    wide_set = jax.ShapeDtypeStruct(tokens.shape, F32)
    for m in range(micro_count):
        keep, arrived, crossed = backs[m]
        (d_tokens,) = by_rows(
            "finish",
            finish_kernel,
            m,
            mods,
            [(tokens, True), (keep, False), (arrived, False), (crossed, False), middles[m][0]],
            [wide_set],
            before=d_tokens,
        )
    sides = feed_total[:, : 2 * hid], feed_total[:, 2 * hid :]
    feed_far = swap_far(after(pick(far, sides[1], sides[0]), crossed))
    total = pick(far, sides[0], sides[1]).astype(F32) + feed_far.astype(F32)
    pieces = jnp.split(total, 2 * hid // CHUNK, axis=1)
    g_up = jnp.concatenate(pieces[0::2], axis=1)
    g_down = jnp.concatenate(pieces[1::2], axis=1).T
    current, sent = halves(by_bits(g_last), 0, falling)
    swapped = swap_dp(sent, 0)
    current = jnp.concatenate(
        [out_keep + out_half.astype(F32), current + swapped.astype(F32)], axis=-1
    )
    for bit in rising[1:]:
        if bit == count - 1:
            current = after(current, crossed)
        current, sent = halves(current, bit, falling[: count - bit])
        current = current + swap_dp(sent, bit).astype(F32)
    g_out = current[:, :part].T
    g_qkv = current[:, part:]

    d_mods = jnp.stack(mod_grads)
    d_mods = after(d_mods + swap_far(d_mods), g_last)
    d_mods = d_mods + swap_near(d_mods)
    all_mods = gather_relative(
        d_mods, lambda value, bit: after(value, swapped) if bit == 1 else value
    ).reshape(-1, d_mods.shape[1])
    g_ada = lax.dot_general(
        cond.astype(F32),
        all_mods,
        TN,
        precision=lax.Precision.HIGHEST,
        preferred_element_type=F32,
    )
    g_bias = lax.dynamic_slice_in_dim(jnp.sum(all_mods, axis=0), device * bias_size, bias_size)
    return (
        output,
        d_tokens,
        g_qkv,
        g_out,
        g_up,
        g_down,
        g_ada,
        g_bias,
    )


def solution(mesh):
    return jax.shard_map(
        per_device,
        mesh=mesh,
        in_specs=(
            P(None, ("dp", "tensor"), None),
            P(None, "dp"),
            P(None, "dp"),
            P(None, ("dp", "tensor"), None),
            P("dp", "tensor"),
            P("tensor", "dp"),
            P("dp", "tensor"),
            P("tensor", "dp"),
            P(("dp", "tensor"), None),
            P(("dp", "tensor")),
        ),
        out_specs=(
            P(None, ("dp", "tensor"), None),
            P(None, ("dp", "tensor"), None),
            P("dp", "tensor"),
            P("tensor", "dp"),
            P("dp", "tensor"),
            P("tensor", "dp"),
            P(("dp", "tensor"), None),
            P(("dp", "tensor")),
        ),
        check_vma=False,
    )
```

profile of v0, /device:TPU:0, one launch (start us, length us, event | category | flops | bytes accessed | tf_op | source)
XLA Modules:
  0.0 432.4 jit_solution(6557763300970275251)
XLA Ops:
  8.0 3.0 collective-permute-start
  11.0 2.6 collective-permute-start.1
  13.6 2.1 slice_bitcast_fusion.3.t0
  23.4 1.6 collective-permute-start.5
  25.5 4.9 %collective-permute-done.2 = f32[2,2]{1,0:T(2,128)S(1)} collective-permute-done((f32[2,2]{1,0:T(2,128)S(1)}, f32[2,2]{1,0:T(2,128)S(1)}, u32[]{:S(2)}, u32[]{:S(2)}) %collective-permute-start.2) | collective-permute-done | bytes 48 | tf_op jit(solution)/shard_map/ppermute | solution.py:42
  30.7 4.1 collective-permute-done.3
  36.4 2.0 mod_terms.1
  40.1 4.6 %collective-permute-done.6 = f32[2,2,2,4608]{3,2,0,1:T(2,128)S(1)} collective-permute-done((f32[2,2,2,4608]{3,2,0,1:T(2,128)S(1)}, f32[2,2,2,4608]{3,2,0,1:T(2,128)S(1)}, u32[]{:S(2)}, u32[]{:S(2)}) %collective-permute-start.6) | collective-permute-done | bytes 147488 | tf_op jit(solution)/shard_map/ppermute | solution.py:42
  44.8 1.7 collective-permute-start.7
  46.5 2.8 collective-permute-done.7
  49.7 4.5 %collective-permute-done.8 = f32[2,4608]{1,0:T(2,128)S(1)} collective-permute-done((f32[2,4608]{1,0:T(2,128)S(1)}, f32[2,4608]{1,0:T(2,128)S(1)}, u32[]{:S(2)}, u32[]{:S(2)}) %collective-permute-start.8) | collective-permute-done | bytes 36896 | tf_op jit(solution)/shard_map/ppermute | solution.py:42
  55.4 7.8 %collective-permute-done.9 = bf16[2,2,96,576]{3,2,0,1:T(8,128)(2,1)S(1)} collective-permute-done((bf16[2,2,96,576]{3,2,0,1:T(8,128)(2,1)S(1)}, bf16[2,2,96,576]{3,2,0,1:T(8,128)(2,1)S(1)}, u32[]{:S(2)}, u32[]{:S(2)}) %collective-permute-start.9) | collective-permute-done | bytes 442400 | tf_op jit(solution)/shard_map/ppermute | solution.py:42
  64.5 3.0 collective-permute-done.11
  70.2 30.4 %attend.2 = (bf16[2048,768]{1,0:T(8,128)(2,1)}, bf16[576,2048]{1,0:T(8,128)(2,1)S(1)}, bf16[192,1024]{1,0:T(8,128)(2,1)S(1)}, bf16[192,1024]{1,0:T(8,128)(2,1)S(1)}, f32[3,1,2048]{2,1,0:T(1,128)S(1)}) custom-call(s32[4]{0:T(128)S(1)} %get-tuple-element.235.lo_ref, s32[4]{0:T(128)S(1)} %get-tuple-element.234.hi_ref, s32[1]{0:T(128)} %bitcast.30.place_ref, ...), custom_call_target="tpu_custom_call" | custom-call | flops 30198988800 | bytes 12582912 | tf_op jit(solution)/shard_map/attend/pallas_call | solution.py:372
  107.2 24.0 %attend.3 = (bf16[2048,768]{1,0:T(8,128)(2,1)}, bf16[576,2048]{1,0:T(8,128)(2,1)S(1)}, bf16[192,1024]{1,0:T(8,128)(2,1)S(1)}, bf16[192,1024]{1,0:T(8,128)(2,1)S(1)}, f32[3,1,2048]{2,1,0:T(1,128)S(1)}) custom-call(s32[4]{0:T(128)S(1)} %copy-done.48, s32[4]{0:T(128)S(1)} %copy-done.47, s32[1]{0:T(128)} %bitcast.30.place_ref, ...), custom_call_target="tpu_custom_call" | custom-call | flops 30198988800 | bytes 12582912 | tf_op jit(solution)/shard_map/attend/pallas_call | solution.py:372
  134.8 11.4 %all-gather.3.cloned.1.call-done = bf16[1536,1728]{1,0:T(8,128)(2,1)} async-done(((bf16[96,1728]{1,0:T(8,128)(2,1)}), bf16[1536,1728]{1,0:T(8,128)(2,1)}) %all-gather.3.cloned.1.call-update) | async-done | bytes 5308432 | tf_op jit(solution)/shard_map/all_gather | solution.py:865
  146.3 2.6 copy-done.1
  151.0 2.3 collective-permute-done.18.arr_ref
  157.8 1.6 collective-permute-start.21
  161.7 22.2 %feed.2 = (f32[512,768]{1,0:T(8,128)S(1)}, bf16[512,768]{1,0:T(8,128)(2,1)}, f32[512,768]{1,0:T(8,128)S(1)}, bf16[512,768]{1,0:T(8,128)(2,1)S(1)}, f32[768,3072]{1,0:T(8,128)}) custom-call(bf16[512,768]{1,0:T(8,128)(2,1)S(1)} %copy-done.56, bf16[512,768]{1,0:T(8,128)(2,1)S(1)} %collective-permute-done.19.n1, bf16[512,768]{1,0:T(8,128)(2,1)S(1)} %copy-done.58, ...), custom_call_target="tpu_custom_call" | custom-call | flops 14495514624 | bytes 14155776 | tf_op jit(solution)/shard_map/feed/pallas_call | solution.py:550
  189.7 2.6 after_feed.2
  195.8 2.0 out_back.2
  200.2 22.1 %feed.3 = (f32[512,768]{1,0:T(8,128)S(1)}, bf16[512,768]{1,0:T(8,128)(2,1)S(1)}, f32[512,768]{1,0:T(8,128)S(1)}, bf16[512,768]{1,0:T(8,128)(2,1)S(1)}, bf16[768,3072]{1,0:T(8,128)(2,1)}) custom-call(bf16[512,768]{1,0:T(8,128)(2,1)S(1)} %get-tuple-element.138.n0, bf16[512,768]{1,0:T(8,128)(2,1)S(1)} %collective-permute-done.26.n1, ...), custom_call_target="tpu_custom_call" | custom-call | flops 14495514624 | bytes 14155776 | tf_op jit(solution)/shard_map/feed/pallas_call | solution.py:550
  222.9 1.8 collective-permute-done.29.b1_ref
  225.8 3.0 after_feed.3
  232.5 2.6 copy-done.2
  236.3 4.3 %out_back.3 = (bf16[192,1024]{1,0:T(8,128)(2,1)S(1)}, bf16[192,1024]{1,0:T(8,128)(2,1)}, f32[768,192]{1,0:T(8,128)S(1)}, bf16[768,192]{1,0:T(8,128)(2,1)S(1)}) custom-call(s32[1]{0:T(128)} %bitcast.30.place_ref, bf16[512,768]{1,0:T(8,128)(2,1)} %get-tuple-element.152.g0_ref, bf16[512,768]{1,0:T(8,128)(2,1)} %collective-permute-done.31.g1_ref, ...), custom_call_target="tpu_custom_call" | custom-call | flops 2415919104 | bytes 3145728 | tf_op jit(solution)/shard_map/out_back/pallas_call | solution.py:671
  241.4 1.7 collective-permute-start.34
  243.5 47.3 %attend_back.2 = (f32[2,512,768]{2,1,0:T(8,128)}, bf16[2,512,768]{2,1,0:T(8,128)(2,1)}, bf16[576,2048]{1,0:T(8,128)(2,1)}, f32[2,768]{1,0:T(2,128)S(1)}) custom-call(s32[8]{0:T(128)S(1)} %copy-done.46, s32[8]{0:T(128)S(1)} %copy-done.45, s32[1]{0:T(128)} %bitcast.30.place_ref, bf16[576,2048]{1,0:T(8,128)(2,1)} %copy-done.71, ...), custom_call_target="tpu_custom_call" | custom-call | flops 45298483200 | bytes 12582912 | tf_op jit(solution)/shard_map/attend_back/pallas_call | solution.py:428
  292.3 6.6 %project_grad.2.rest_0_ = f32[768,576]{1,0:T(8,128)} custom-call(bf16[2048,768]{1,0:T(8,128)(2,1)} %get-tuple-element.168.normed_ref, bf16[576,2048]{1,0:T(8,128)(2,1)} %get-tuple-element.169.back_ref), custom_call_target="tpu_custom_call" | custom-call | flops 36238786560 | bytes 6291456 | tf_op jit(solution)/shard_map/project_grad/pallas_call | solution.py:343
  301.0 2.3 fusion
  303.3 1.8 collective-permute-start.35
  305.1 39.8 %attend_back.3 = (f32[2,512,768]{2,1,0:T(8,128)}, bf16[2,512,768]{2,1,0:T(8,128)(2,1)}, bf16[576,2048]{1,0:T(8,128)(2,1)}, f32[2,768]{1,0:T(2,128)S(1)}) custom-call(s32[8]{0:T(128)S(1)} %copy-done.44, s32[8]{0:T(128)S(1)} %copy-done.43, s32[1]{0:T(128)} %bitcast.30.place_ref, bf16[576,2048]{1,0:T(8,128)(2,1)} %copy-done.70, ...), custom_call_target="tpu_custom_call" | custom-call | flops 45298483200 | bytes 12582912 | tf_op jit(solution)/shard_map/attend_back/pallas_call | solution.py:428
  346.5 7.2 %project_grad.3 = f32[768,576]{1,0:T(8,128)} custom-call(bf16[2048,768]{1,0:T(8,128)(2,1)} %get-tuple-element.185.normed_ref, bf16[576,2048]{1,0:T(8,128)(2,1)} %get-tuple-element.186.back_ref, f32[768,576]{1,0:T(8,128)} %project_grad.2.rest_0_), custom_call_target="tpu_custom_call" | custom-call | flops 36238786560 | bytes 6291456 | tf_op jit(solution)/shard_map/project_grad/pallas_call | solution.py:343
  353.8 2.5 fusion.1
  357.6 1.6 fusion.5
  359.2 2.1 collective-permute-start.39
  361.6 11.0 %collective-permute-done.39 = bf16[2,2,96,576]{3,2,1,0:T(8,128)(2,1)S(1)} collective-permute-done((bf16[2,2,96,576]{3,2,1,0:T(8,128)(2,1)S(1)}, bf16[2,2,96,576]{3,2,1,0:T(8,128)(2,1)S(1)}, u32[]{:S(2)}, u32[]{:S(2)}) %collective-permute-start.39) | collective-permute-done | bytes 442400 | tf_op jit(solution)/shard_map/ppermute | solution.py:42
  372.6 10.7 %collective-permute-start.46 = (f32[2,2,4608]{2,1,0:T(2,128)S(1)}, f32[2,2,4608]{2,1,0:T(2,128)S(1)}, u32[]{:S(2)}, u32[]{:S(2)}) collective-permute-start(f32[2,2,4608]{2,1,0:T(2,128)S(1)} %pad_maximum_fusion.8), channel_id=1, source_target_pairs={{0,8},{4,12},{8,0},{12,4},{16,24},{20,28},{24,16},{28,20},{1,9},{5... | collective-permute-start | bytes 221192 | tf_op jit(solution)/shard_map/ppermute | solution.py:42
  385.0 1.9 copy-done.5
  388.3 2.1 finish.2.rest_0_
  391.2 3.8 collective-permute-start.47
  397.0 2.0 collective-permute-start.40
  406.6 1.9 fusion.21
  408.5 1.7 fusion.4
  412.4 3.0 finish.3
  417.3 1.9 collective-permute-done.41
  421.9 1.7 collective-permute-done.42
  (368 shorter events, 84.6 us)
Async XLA Ops:
  7.2 139.1 %all-gather.3.cloned.1.call-start = ((), (), s32[]{:S(2)}) async-start(), calls=%async_computation.2 | async-start | bytes 5849088 | tf_op jit(solution)/shard_map/all_gather | solution.py:865
  8.0 15.2 %collective-permute-start = (f32[2]{0:T(128)S(1)}, f32[2]{0:T(128)S(1)}, u32[]{:S(2)}, u32[]{:S(2)}) collective-permute-start(f32[2]{0:T(128)S(1)} %get-tuple-element.267), channel_id=1, source_target_pairs={{0,4},{4,0},{8,12},{12,8},{16,20},{20,16},{24,28},{28,24},{1,5},{5... | collective-permute-start | bytes 32 | tf_op jit(solution)/shard_map/ppermute | solution.py:42
  11.0 12.3 %collective-permute-start.1 = (bf16[96,576]{1,0:T(8,128)(2,1)}, bf16[96,576]{1,0:T(8,128)(2,1)S(1)}, u32[]{:S(2)}, u32[]{:S(2)}) collective-permute-start(bf16[96,576]{1,0:T(8,128)(2,1)} %param.14), channel_id=1, source_target_pairs={{0,16},{4,20},{8,24},{12,28},{16,0},{20,4},{24,8},{28,12},{1,17},{... | collective-permute-start | bytes 331784 | tf_op jit(solution)/shard_map/ppermute | solution.py:42
  15.6 20.1 %collective-permute-start.4 = (bf16[512,768]{1,0:T(8,128)(2,1)}, bf16[512,768]{1,0:T(8,128)(2,1)S(1)}, u32[]{:S(2)}, u32[]{:S(2)}) collective-permute-start(bf16[512,768]{1,0:T(8,128)(2,1)} %slice_bitcast_fusion.3.t0), channel_id=1, source_target_pairs={{0,2},{1,3},{2,0},{3,1},{4,6},{5,7},{6,4},{7,5},{8,10},{9,11},{10,... | collective-permute-start | bytes 2359304 | tf_op jit(solution)/shard_map/ppermute | solution.py:33
  23.4 12.2 %collective-permute-start.5 = (bf16[2,96,576]{2,1,0:T(8,128)(2,1)S(1)}, bf16[2,96,576]{2,1,0:T(8,128)(2,1)S(1)}, u32[]{:S(2)}, u32[]{:S(2)}) collective-permute-start(bf16[2,96,576]{2,1,0:T(8,128)(2,1)S(1)} %pad_maximum_fusion.6), channel_id=1, source_target_pairs={{0,8},{4,12},{8,0},{12,4},{16,24},{20,28},{24,16},{28,20},{1,9},{5... | collective-permute-start | bytes 663560 | tf_op jit(solution)/shard_map/ppermute | solution.py:42
  25.0 5.3 %collective-permute-start.2 = (f32[2,2]{1,0:T(2,128)S(1)}, f32[2,2]{1,0:T(2,128)S(1)}, u32[]{:S(2)}, u32[]{:S(2)}) collective-permute-start(f32[2,2]{1,0:T(2,128)S(1)} %pad_maximum_fusion.14), channel_id=1, source_target_pairs={{0,8},{4,12},{8,0},{12,4},{16,24},{20,28},{24,16},{28,20},{1,9},{5... | collective-permute-start | bytes 56 | tf_op jit(solution)/shard_map/ppermute | solution.py:42
  30.4 4.5 %collective-permute-start.3 = (f32[2,2,2]{2,1,0:T(2,128)S(1)}, f32[2,2,2]{2,1,0:T(2,128)S(1)}, u32[]{:S(2)}, u32[]{:S(2)}) collective-permute-start(f32[2,2,2]{2,1,0:T(2,128)S(1)} %pad_maximum_fusion.13), channel_id=1, source_target_pairs={{0,16},{4,20},{8,24},{12,28},{16,0},{20,4},{24,8},{28,12},{1,17},{... | collective-permute-start | bytes 104 | tf_op jit(solution)/shard_map/ppermute | solution.py:42
  39.5 5.2 %collective-permute-start.6 = (f32[2,2,2,4608]{3,2,0,1:T(2,128)S(1)}, f32[2,2,2,4608]{3,2,0,1:T(2,128)S(1)}, u32[]{:S(2)}, u32[]{:S(2)}) collective-permute-start(f32[2,2,2,4608]{3,2,0,1:T(2,128)S(1)} %bitcast.163), channel_id=1, source_target_pairs={{0,4},{4,0},{8,12},{12,8},{16,20},{20,16},{24,28},{28,24},{1,5},{5... | collective-permute-start | bytes 442376 | tf_op jit(solution)/shard_map/ppermute | solution.py:42
  44.8 4.4 %collective-permute-start.7 = (f32[2,2,4608]{2,1,0:T(2,128)S(1)}, f32[2,2,4608]{2,1,0:T(2,128)S(1)}, u32[]{:S(2)}, u32[]{:S(2)}) collective-permute-start(f32[2,2,4608]{2,1,0:T(2,128)S(1)} %slice_bitcast_fusion.7), channel_id=1, source_target_pairs={{0,8},{4,12},{8,0},{12,4},{16,24},{20,28},{24,16},{28,20},{1,9},{5... | collective-permute-start | bytes 221192 | tf_op jit(solution)/shard_map/ppermute | solution.py:42
  49.3 4.9 %collective-permute-start.8 = (f32[2,4608]{1,0:T(2,128)S(1)}, f32[2,4608]{1,0:T(2,128)S(1)}, u32[]{:S(2)}, u32[]{:S(2)}) collective-permute-start(f32[2,4608]{1,0:T(2,128)S(1)} %slice_bitcast_fusion.9), channel_id=1, source_target_pairs={{0,16},{4,20},{8,24},{12,28},{16,0},{20,4},{24,8},{28,12},{1,17},{... | collective-permute-start | bytes 110600 | tf_op jit(solution)/shard_map/ppermute | solution.py:42
  54.3 361.2 %reduce-scatter.2.cloned.1.call-start = ((), (), s32[]{:S(2)}) async-start(), calls=%async_computation.1 | async-start | bytes 5308416 | tf_op jit(solution)/shard_map/reduce_scatter | solution.py:955
  54.3 8.9 %collective-permute-start.9 = (bf16[2,2,96,576]{3,2,0,1:T(8,128)(2,1)S(1)}, bf16[2,2,96,576]{3,2,0,1:T(8,128)(2,1)S(1)}, u32[]{:S(2)}, u32[]{:S(2)}) collective-permute-start(bf16[2,2,96,576]{3,2,0,1:T(8,128)(2,1)S(1)} %pad_maximum_fusion.2), channel_id=1, source_target_pairs={{0,4},{4,0},{8,12},{12,8},{16,20},{20,16},{24,28},{28,24},{1,5},{5... | collective-permute-start | bytes 1327112 | tf_op jit(solution)/shard_map/ppermute | solution.py:42
  54.9 8.6 %collective-permute-start.10 = (bf16[512,768]{1,0:T(8,128)(2,1)S(1)}, bf16[512,768]{1,0:T(8,128)(2,1)}, u32[]{:S(2)}, u32[]{:S(2)}) collective-permute-start(bf16[512,768]{1,0:T(8,128)(2,1)S(1)} %collective-permute-done.4.t2), channel_id=1, source_target_pairs={{0,1},{1,0},{2,3},{3,2},{4,5},{5,4},{6,7},{7,6},{8,9},{9,8},{10,11... | collective-permute-start | bytes 2359304 | tf_op jit(solution)/shard_map/ppermute | solution.py:37
  54.9 15.2 %collective-permute-start.15 = (bf16[512,768]{1,0:T(8,128)(2,1)}, bf16[512,768]{1,0:T(8,128)(2,1)}, u32[]{:S(2)}, u32[]{:S(2)}) collective-permute-start(bf16[512,768]{1,0:T(8,128)(2,1)} %slice_bitcast_fusion.3.t0), channel_id=1, source_target_pairs={{0,1},{1,0},{2,3},{3,2},{4,5},{5,4},{6,7},{7,6},{8,9},{9,8},{10,11... | collective-permute-start | bytes 2359304 | tf_op jit(solution)/shard_map/ppermute | solution.py:37
  63.5 4.0 collective-permute-start.11
  69.0 35.0 %collective-permute-start.13 = (bf16[512,768]{1,0:T(8,128)(2,1)S(1)}, bf16[512,768]{1,0:T(8,128)(2,1)S(1)}, u32[]{:S(2)}, u32[]{:S(2)}) collective-permute-start(bf16[512,768]{1,0:T(8,128)(2,1)S(1)} %slice_bitcast_fusion.2.t0), channel_id=1, source_target_pairs={{0,1},{1,0},{2,3},{3,2},{4,5},{5,4},{6,7},{7,6},{8,9},{9,8},{10,11... | collective-permute-start | bytes 2359304 | tf_op jit(solution)/shard_map/ppermute | solution.py:37
  69.2 33.5 %collective-permute-start.14 = (bf16[512,768]{1,0:T(8,128)(2,1)S(1)}, bf16[512,768]{1,0:T(8,128)(2,1)S(1)}, u32[]{:S(2)}, u32[]{:S(2)}) collective-permute-start(bf16[512,768]{1,0:T(8,128)(2,1)S(1)} %slice_bitcast_fusion.2.t0), channel_id=1, source_target_pairs={{0,2},{1,3},{2,0},{3,1},{4,6},{5,7},{6,4},{7,5},{8,10},{9,11},{10,... | collective-permute-start | bytes 2359304 | tf_op jit(solution)/shard_map/ppermute | solution.py:33
  102.7 2.4 collective-permute-start.16
  102.8 31.3 %collective-permute-start.17 = (bf16[192,1024]{1,0:T(8,128)(2,1)S(1)}, bf16[192,1024]{1,0:T(8,128)(2,1)S(1)}, u32[]{:S(2)}, u32[]{:S(2)}) collective-permute-start(bf16[192,1024]{1,0:T(8,128)(2,1)S(1)} %get-tuple-element.114.far_ref), channel_id=1, source_target_pairs={{0,2},{1,3},{2,0},{3,1},{4,6},{5,7},{6,4},{7,5},{8,10},{9,11},{10,... | collective-permute-start | bytes 1179656 | tf_op jit(solution)/shard_map/ppermute | solution.py:33
  150.9 2.4 collective-permute-start.18
  155.4 3.9 collective-permute-start.19
  156.5 2.9 collective-permute-start.20
  157.8 28.5 %collective-permute-start.21 = (bf16[192,1024]{1,0:T(8,128)(2,1)S(1)}, bf16[192,1024]{1,0:T(8,128)(2,1)S(1)}, u32[]{:S(2)}, u32[]{:S(2)}) collective-permute-start(bf16[192,1024]{1,0:T(8,128)(2,1)S(1)} %copy-done.60), channel_id=1, source_target_pairs={{0,2},{1,3},{2,0},{3,1},{4,6},{5,7},{6,4},{7,5},{8,10},{9,11},{10,... | collective-permute-start | bytes 1179656 | tf_op jit(solution)/shard_map/ppermute | solution.py:33
  186.2 2.6 collective-permute-start.23
  186.4 3.3 collective-permute-start.24
  187.9 5.8 %collective-permute-start.22 = (bf16[512,768]{1,0:T(8,128)(2,1)S(1)}, bf16[512,768]{1,0:T(8,128)(2,1)S(1)}, u32[]{:S(2)}, u32[]{:S(2)}) collective-permute-start(bf16[512,768]{1,0:T(8,128)(2,1)S(1)} %get-tuple-element.128), channel_id=1, source_target_pairs={{0,1},{1,0},{2,3},{3,2},{4,5},{5,4},{6,7},{7,6},{8,9},{9,8},{10,11... | collective-permute-start | bytes 2359304 | tf_op jit(solution)/shard_map/ppermute | solution.py:37
  193.6 2.3 collective-permute-start.25
  194.7 4.9 %collective-permute-start.27 = (bf16[512,768]{1,0:T(8,128)(2,1)S(1)}, bf16[512,768]{1,0:T(8,128)(2,1)S(1)}, u32[]{:S(2)}, u32[]{:S(2)}) collective-permute-start(bf16[512,768]{1,0:T(8,128)(2,1)S(1)} %get-tuple-element.139.g0), channel_id=1, source_target_pairs={{0,1},{1,0},{2,3},{3,2},{4,5},{5,4},{6,7},{7,6},{8,9},{9,8},{10,11... | collective-permute-start | bytes 2359304 | tf_op jit(solution)/shard_map/ppermute | solution.py:37
  197.9 2.4 collective-permute-start.26
  198.1 24.2 %collective-permute-start.28 = (bf16[192,1024]{1,0:T(8,128)(2,1)S(1)}, bf16[192,1024]{1,0:T(8,128)(2,1)S(1)}, u32[]{:S(2)}, u32[]{:S(2)}) collective-permute-start(bf16[192,1024]{1,0:T(8,128)(2,1)S(1)} %get-tuple-element.137), channel_id=1, source_target_pairs={{0,2},{1,3},{2,0},{3,1},{4,6},{5,7},{6,4},{7,5},{8,10},{9,11},{10,... | collective-permute-start | bytes 1179656 | tf_op jit(solution)/shard_map/ppermute | solution.py:33
  222.3 2.4 collective-permute-start.29
  222.5 3.3 collective-permute-start.30
  229.9 2.6 collective-permute-start.31
  241.4 59.6 %collective-permute-start.34 = (bf16[192,1024]{1,0:T(8,128)(2,1)}, bf16[192,1024]{1,0:T(8,128)(2,1)}, u32[]{:S(2)}, u32[]{:S(2)}) collective-permute-start(bf16[192,1024]{1,0:T(8,128)(2,1)} %get-tuple-element.158), channel_id=1, source_target_pairs={{0,2},{1,3},{2,0},{3,1},{4,6},{5,7},{6,4},{7,5},{8,10},{9,11},{10,... | collective-permute-start | bytes 1179656 | tf_op jit(solution)/shard_map/ppermute | solution.py:33
  243.1 47.7 %collective-permute-start.32 = (bf16[768,192]{1,0:T(8,128)(2,1)S(1)}, bf16[768,192]{1,0:T(8,128)(2,1)S(1)}, u32[]{:S(2)}, u32[]{:S(2)}) collective-permute-start(bf16[768,192]{1,0:T(8,128)(2,1)S(1)} %get-tuple-element.165), channel_id=1, source_target_pairs={{0,2},{1,3},{2,0},{3,1},{4,6},{5,7},{6,4},{7,5},{8,10},{9,11},{10,... | collective-permute-start | bytes 884744 | tf_op jit(solution)/shard_map/ppermute | solution.py:33
  290.8 10.2 %collective-permute-start.33 = (bf16[2,512,768]{2,1,0:T(8,128)(2,1)}, bf16[2,512,768]{2,1,0:T(8,128)(2,1)S(1)}, u32[]{:S(2)}, u32[]{:S(2)}) collective-permute-start(bf16[2,512,768]{2,1,0:T(8,128)(2,1)} %get-tuple-element.167), channel_id=1, source_target_pairs={{0,1},{1,0},{2,3},{3,2},{4,5},{5,4},{6,7},{7,6},{8,9},{9,8},{10,11... | collective-permute-start | bytes 4718600 | tf_op jit(solution)/shard_map/ppermute | solution.py:37
  292.1 52.8 %collective-permute-start.36 = (bf16[2,2,96,192]{3,2,1,0:T(8,128)(2,1)}, bf16[2,2,96,192]{3,2,1,0:T(8,128)(2,1)}, u32[]{:S(2)}, u32[]{:S(2)}) collective-permute-start(bf16[2,2,96,192]{3,2,1,0:T(8,128)(2,1)} %fusion.9), channel_id=1, source_target_pairs={{0,4},{4,0},{8,12},{12,8},{16,20},{20,16},{24,28},{28,24},{1,5},{5... | collective-permute-start | bytes 442376 | tf_op jit(solution)/shard_map/ppermute | solution.py:42
  303.3 41.7 %collective-permute-start.35 = (bf16[512,768]{1,0:T(8,128)(2,1)S(1)}, bf16[512,768]{1,0:T(8,128)(2,1)S(1)}, u32[]{:S(2)}, u32[]{:S(2)}) collective-permute-start(bf16[512,768]{1,0:T(8,128)(2,1)S(1)} %fusion), channel_id=1, source_target_pairs={{0,2},{1,3},{2,0},{3,1},{4,6},{5,7},{6,4},{7,5},{8,10},{9,11},{10,... | collective-permute-start | bytes 2359304 | tf_op jit(solution)/shard_map/ppermute | solution.py:33
  345.8 7.9 %collective-permute-start.37 = (bf16[2,512,768]{2,1,0:T(8,128)(2,1)}, bf16[2,512,768]{2,1,0:T(8,128)(2,1)S(1)}, u32[]{:S(2)}, u32[]{:S(2)}) collective-permute-start(bf16[2,512,768]{2,1,0:T(8,128)(2,1)} %get-tuple-element.181), channel_id=1, source_target_pairs={{0,1},{1,0},{2,3},{3,2},{4,5},{5,4},{6,7},{7,6},{8,9},{9,8},{10,11... | collective-permute-start | bytes 4718600 | tf_op jit(solution)/shard_map/ppermute | solution.py:37
  345.9 7.8 %collective-permute-start.43 = (f32[2,4608]{1,0:T(2,128)S(1)}, f32[2,4608]{1,0:T(2,128)S(1)}, u32[]{:S(2)}, u32[]{:S(2)}) collective-permute-start(f32[2,4608]{1,0:T(2,128)S(1)} %pad_maximum_fusion.9), channel_id=1, source_target_pairs={{0,2},{1,3},{2,0},{3,1},{4,6},{5,7},{6,4},{7,5},{8,10},{9,11},{10,... | collective-permute-start | bytes 110600 | tf_op jit(solution)/shard_map/ppermute | solution.py:33
  357.5 4.0 collective-permute-start.45
  359.2 13.4 %collective-permute-start.39 = (bf16[2,2,96,576]{3,2,1,0:T(8,128)(2,1)S(1)}, bf16[2,2,96,576]{3,2,1,0:T(8,128)(2,1)S(1)}, u32[]{:S(2)}, u32[]{:S(2)}) collective-permute-start(bf16[2,2,96,576]{3,2,1,0:T(8,128)(2,1)S(1)} %fusion.5), channel_id=1, source_target_pairs={{0,4},{4,0},{8,12},{12,8},{16,20},{20,16},{24,28},{28,24},{1,5},{5... | collective-permute-start | bytes 1327112 | tf_op jit(solution)/shard_map/ppermute | solution.py:42
  372.6 17.8 %collective-permute-start.46 = (f32[2,2,4608]{2,1,0:T(2,128)S(1)}, f32[2,2,4608]{2,1,0:T(2,128)S(1)}, u32[]{:S(2)}, u32[]{:S(2)}) collective-permute-start(f32[2,2,4608]{2,1,0:T(2,128)S(1)} %pad_maximum_fusion.8), channel_id=1, source_target_pairs={{0,8},{4,12},{8,0},{12,4},{16,24},{20,28},{24,16},{28,20},{1,9},{5... | collective-permute-start | bytes 221192 | tf_op jit(solution)/shard_map/ppermute | solution.py:42
  384.7 25.5 %collective-permute-start.38 = (bf16[512,768]{1,0:T(8,128)(2,1)}, bf16[512,768]{1,0:T(8,128)(2,1)}, u32[]{:S(2)}, u32[]{:S(2)}) collective-permute-start(bf16[512,768]{1,0:T(8,128)(2,1)} %fusion.1), channel_id=1, source_target_pairs={{0,2},{1,3},{2,0},{3,1},{4,6},{5,7},{6,4},{7,5},{8,10},{9,11},{10,... | collective-permute-start | bytes 2359304 | tf_op jit(solution)/shard_map/ppermute | solution.py:33
  391.2 10.4 %collective-permute-start.47 = (f32[2,2,2,4608]{3,2,1,0:T(2,128)}, f32[2,2,2,4608]{3,2,1,0:T(2,128)S(1)}, u32[]{:S(2)}, u32[]{:S(2)}) collective-permute-start(f32[2,2,2,4608]{3,2,1,0:T(2,128)} %get-tuple-element.251), channel_id=1, source_target_pairs={{0,16},{4,20},{8,24},{12,28},{16,0},{20,4},{24,8},{28,12},{1,17},{... | collective-permute-start | bytes 442376 | tf_op jit(solution)/shard_map/ppermute | solution.py:42
  397.0 11.4 %collective-permute-start.40 = (bf16[2,96,768]{2,1,0:T(8,128)(2,1)}, bf16[2,96,768]{2,1,0:T(8,128)(2,1)}, u32[]{:S(2)}, u32[]{:S(2)}) collective-permute-start(bf16[2,96,768]{2,1,0:T(8,128)(2,1)} %fusion.6), channel_id=1, source_target_pairs={{0,8},{4,12},{8,0},{12,4},{16,24},{20,28},{24,16},{28,20},{1,9},{5... | collective-permute-start | bytes 884744 | tf_op jit(solution)/shard_map/ppermute | solution.py:42
  410.2 9.0 %collective-permute-start.41 = (bf16[96,768]{1,0:T(8,128)(2,1)S(1)}, bf16[96,768]{1,0:T(8,128)(2,1)S(1)}, u32[]{:S(2)}, u32[]{:S(2)}) collective-permute-start(bf16[96,768]{1,0:T(8,128)(2,1)S(1)} %fusion.10), channel_id=1, source_target_pairs={{0,16},{4,20},{8,24},{12,28},{16,0},{20,4},{24,8},{28,12},{1,17},{... | collective-permute-start | bytes 442376 | tf_op jit(solution)/shard_map/ppermute | solution.py:42
  416.6 6.9 %collective-permute-start.42 = (bf16[96,1536]{1,0:T(8,128)(2,1)S(1)}, bf16[96,1536]{1,0:T(8,128)(2,1)S(1)}, u32[]{:S(2)}, u32[]{:S(2)}) collective-permute-start(bf16[96,1536]{1,0:T(8,128)(2,1)S(1)} %broadcast_select_fusion), channel_id=1, source_target_pairs={{0,2},{1,3},{2,0},{3,1},{4,6},{5,7},{6,4},{7,5},{8,10},{9,11},{10,... | collective-permute-start | bytes 884744 | tf_op jit(solution)/shard_map/ppermute | solution.py:33
  (100 other events, 1197.8 us)
Sparse Core Ops, SparseCore 0:
  54.4 91.8 all-gather.2
  230.8 97.1 reduce-scatter.1
where the time goes:
time: 440 us; the launch traced here: 432 us
  Pallas kernels  223 us (51%)
  waiting for transfers between devices  71 us (16%)
  starting transfers between devices  47.2 us (11%)
  local copies, waits for them, and re-layouts  45.4 us (10%)
  other arithmetic  28.6 us (6%)
  between operations  15.7 us (4%)
    pallas_call x2, Pallas kernels, attend_back(): pl.pallas_call(functools.partial(attend_back_kernel, bq, bk, heads), grid...  87 us
    pallas_call x2, Pallas kernels, attend(): pl.pallas_call(functools.partial(attend_kernel, m, bq, bk, heads), grid_s...  54.5 us
    pallas_call x2, Pallas kernels, feed(): pl.pallas_call(functools.partial(feed_kernel, 4, add), grid=(2 * steps,),...  44.3 us
    ppermute x16, waiting for transfers between devices, swap_dp(): return lax.ppermute(value, 'dp', [(i, i ^ 1 << bit) for i in range(count)])  42.3 us
    unnamed x207, local copies, waits for them, and re-layouts  36.3 us
    ppermute x16, starting transfers between devices, swap_dp(): return lax.ppermute(value, 'dp', [(i, i ^ 1 << bit) for i in range(count)])  29.9 us
    pallas_call x2, Pallas kernels, project_grad(): pl.pallas_call(functools.partial(project_grad_kernel, add), grid=(4,), in...  13.9 us
    ppermute x12, starting transfers between devices, swap_far(): return lax.ppermute(value, 'tensor', [(i, i ^ 2) for i in range(4)])  13.1 us
  transfers between devices with their start and end apart: 50, of which 24 were waited for; matrix products, arithmetic and copies ran while one was open for 8% of the time, Pallas kernels for 50%

commit v1 on v0

--- a/solution.py
+++ b/solution.py
@@ -251,30 +251,20 @@
         def query_block(i, _):
             columns = pl.ds(pl.multiple_of(i * bq, bq), bq)
             allowed = same_documents(row_ref, col_s, keys, columns, bq)
-            scores = [
-                dot(
-                    k_s[h, keys, :] * jnp.asarray(0.125, BF16),
-                    qkv_ref[3 * HD * h : 3 * HD * h + HD, columns],
-                )
-                for h in range(heads)
-            ]
-            d_chances = [
-                dot(v_s[h, keys, :], dat_s[HD * h : HD * h + HD, columns]) for h in range(heads)
-            ]
-            lows, d_lows = [], []
-            for h in range(heads):
-                chances = jnp.where(
-                    allowed, jnp.exp(scores[h] - lse_ref[h, 0:1, columns]), 0.0
-                )
-                lows.append(chances.astype(BF16))
-                d_lows.append((chances * (d_chances[h] - inner_s[h, 0:1, columns])).astype(BF16))
             for h in range(heads):
                 base = 3 * HD * h
-                dv_s[h, keys, :] += dot(lows[h], g_s[h, columns, :])
-                dk_s[h, keys, :] += dot(d_lows[h], q_s[h, columns, :])
-                dq_s[HD * h : HD * h + HD, columns] += dot(
-                    qkv_ref[base + HD : base + 2 * HD, keys], d_lows[h]
+                head = slice(HD * h, HD * h + HD)
+                scores = dot(
+                    k_s[h, keys, :] * jnp.asarray(0.125, BF16), qkv_ref[base : base + HD, columns]
                 )
+                chances = jnp.where(
+                    allowed, jnp.exp(scores - lse_ref[h, 0:1, columns]), 0.0
+                )
+                d_chances = dot(v_s[h, keys, :], dat_s[head, columns])
+                d_scores = (chances * (d_chances - inner_s[h, 0:1, columns])).astype(BF16)
+                dv_s[h, keys, :] += dot(chances.astype(BF16), g_s[h, columns, :])
+                dk_s[h, keys, :] += dot(d_scores, q_s[h, columns, :])
+                dq_s[head, columns] += dot(qkv_ref[base + HD : base + 2 * HD, keys], d_scores)
             return 0
 
         lax.fori_loop(lo_ref[j], hi_ref[j], query_block, 0)
@@ -593,7 +583,7 @@
 
 
 def out_weights(pack_ref, side, size):
-    return pack_ref[:, pl.ds(side, 1), :, 0:size].reshape(-1, size)
+    return pack_ref[:, pl.ds(side, 1), :, :].reshape(-1, size)
 
 
 def out_kernel(place_ref, own_ref, far_ref, pack_ref, keep_ref, send_ref):
@@ -609,11 +599,6 @@
         ).astype(ref.dtype)
 
 
-def pack_tail(pack):
-    count, _, height, columns = pack.shape
-    return pl.BlockSpec((count, 2, height, CHUNK), lambda i, *_: (0, 0, 0, columns // CHUNK))
-
-
 def out_project(place, own, away, pack):
     size, total = own.shape
     rows, width = total // 2, pack.shape[0] * pack.shape[2]
@@ -622,7 +607,7 @@
         grid_spec=pltpu.PrefetchScalarGridSpec(
             num_scalar_prefetch=1,
             grid=(1,),
-            in_specs=[held(size, total), held(size, total), pack_tail(pack)],
+            in_specs=[held(size, total), held(size, total), held(*pack.shape)],
             out_specs=[held(rows, width), held(rows, width)],
         ),
         out_shape=[
@@ -674,7 +659,7 @@
             num_scalar_prefetch=1,
             grid=(1,),
             in_specs=[held(rows, width)] * 2
-            + [half, half, pack_tail(pack)]
+            + [half, half, held(*pack.shape)]
             + [held(width, size)] * (2 * add),
             out_specs=[half, half, held(width, size), held(width, size)],
         ),
@@ -762,7 +747,9 @@
         cost_estimate=pl.CostEstimate(
             flops=weight * rows * width, bytes_accessed=32 * rows * width, transcendentals=rows
         ),
-        compiler_params=pltpu.CompilerParams(vmem_limit_bytes=16 * 2**20),
+        compiler_params=None
+        if name == "finish"
+        else pltpu.CompilerParams(vmem_limit_bytes=16 * 2**20),
         name=name,
     )(mods, *values, *extra)
 
@@ -828,9 +815,14 @@
         return after(value, states[step])
 
     def with_stamps(value, bit):
-        if bit == count - 1:
-            return after(value, (tables, doc_rows, bounds, pack))
         return advance(value, bit - 1) if bit >= 1 else value
+
+    begun = []
+
+    def with_terms(value, bit):
+        if bit == 0:
+            begun.append(value)
+        return value
 
     ready = tokens[0]
     across = swap_far(ready)
@@ -850,15 +842,14 @@
         jnp.arange(slots)[:, None] == device, b_ada.astype(F32)[None, :], 0.0
     ).reshape(-1)
     terms = mod_terms(advance(after(cond, across), count - 2), w_ada, bias)
-    mods = scatter_relative(terms.reshape(-1, micro_count, terms.shape[1]))
-
-    begun = mods
-    mods = after(advance(mods, count - 1), blocks[0][3])
+    mods = scatter_relative(terms.reshape(-1, micro_count, terms.shape[1]), with_terms)
+
+    mods = after(advance(mods, count - 1), (blocks[0][3], tables, doc_rows, bounds))
     wq = states[-1].reshape(width, -1)
     mods = mods + swap_far(mods)
     mods = mods + swap_near(mods)
 
-    pack = after(pack, begun)
+    pack = after(pack, begun[0])
     groups = [
         [4 * i + 2 * j + c for i in range(lax.axis_size("dp")) for j in range(2)] for c in range(2)
     ]
@@ -882,6 +873,7 @@
         )
         state.append((normed_a, qkv, (att_own, att_away), lse))
 
+    out_pack = pack[..., 2 * hid :]
     every = jax.ShapeDtypeStruct(tokens.shape, BF16)
     wide = jax.ShapeDtypeStruct((rows, width), F32)
     low = jax.ShapeDtypeStruct((rows, width), BF16)
@@ -897,7 +889,7 @@
         att_far = crossing[m]
         if not last:
             att_far = after(att_far, state[m + 1][2][0])
-        keep, send = out_project(place, att_own, att_far, pack)
+        keep, send = out_project(place, att_own, att_far, out_pack)
         branch_a, normed_m, grad_m = by_rows(
             "before_feed",
             before_feed_kernel,
@@ -945,7 +937,7 @@
             sums=4,
         )
         d_att_own, d_att_far, *grads_out = out_back(
-            place, (grad_a, swap_near(grad_a)), att_own, att_far, pack, grads_out,
+            place, (grad_a, swap_near(grad_a)), att_own, att_far, out_pack, grads_out,
             last,
         )
         if m > 0:
@@ -992,16 +984,19 @@
     d_tokens = None
     wide_set = jax.ShapeDtypeStruct(tokens.shape, F32)
     for m in range(micro_count):
-        keep, arrived, crossed = backs[m]
+        keep, arrived, crossing = backs[m]
         (d_tokens,) = by_rows(
             "finish",
             finish_kernel,
             m,
             mods,
-            [(tokens, True), (keep, False), (arrived, False), (crossed, False), middles[m][0]],
+            [(tokens, True), (keep, False), (arrived, False), (crossing, False), middles[m][0]],
             [wide_set],
             before=d_tokens,
         )
+        if m == 0:
+            d_tokens, backs[-1][2] = lax.optimization_barrier((d_tokens, backs[-1][2]))
+            first_done, crossed = d_tokens, backs[-1][2]
     sides = feed_total[:, : 2 * hid], feed_total[:, 2 * hid :]
     feed_far = swap_far(after(pick(far, sides[1], sides[0]), crossed))
     total = pick(far, sides[0], sides[1]).astype(F32) + feed_far.astype(F32)
@@ -1009,12 +1004,12 @@
     g_up = jnp.concatenate(pieces[0::2], axis=1)
     g_down = jnp.concatenate(pieces[1::2], axis=1).T
     current, sent = halves(by_bits(g_last), 0, falling)
-    swapped = swap_dp(sent, 0)
+    swapped = after(swap_dp(sent, 0), first_done)
     current = jnp.concatenate(
         [out_keep + out_half.astype(F32), current + swapped.astype(F32)], axis=-1
     )
     for bit in rising[1:]:
-        if bit == count - 1:
+        if bit == 1:
             current = after(current, crossed)
         current, sent = halves(current, bit, falling[: count - bit])
         current = current + swap_dp(sent, bit).astype(F32)

time: 440 us -> 408 us (0.927); the launches traced: 432 us -> 406 us
  local copies, waits for them, and re-layouts: 45.4 us -> 24.6 us
  Pallas kernels: 223 us -> 240 us
  other arithmetic: 28.6 us -> 18 us
  starting transfers between devices: 47.2 us -> 39 us
    unnamed x207 -> x153, local copies, waits for them, and re-layouts: 36.3 us -> 18.4 us
    ppermute x16, waiting for transfers between devices: 42.3 us -> 31.1 us  [swap_dp(): return lax.ppermute(value, 'dp', [(i, i ^ 1 << bit) for i in range(count)])]
    ppermute x16, starting transfers between devices: 29.9 us -> 19.4 us  [swap_dp(): return lax.ppermute(value, 'dp', [(i, i ^ 1 << bit) for i in range(count)])]
    ppermute x12, waiting for transfers between devices: 4.71 us -> 14.8 us  [swap_far(): return lax.ppermute(value, 'tensor', [(i, i ^ 2) for i in range(4)])]
    pallas_call x2, Pallas kernels: 87 us -> 96.1 us  [attend_back(): pl.pallas_call(functools.partial(attend_back_kernel, bq, bk, heads), grid...]
    pallas_call x2, Pallas kernels: 54.5 us -> 59.6 us  [attend(): pl.pallas_call(functools.partial(attend_kernel, m, bq, bk, heads), grid_s...]
  transfers between devices with their start and end apart: 50 -> 50, of which waited for: 24 -> 25; matrix products, arithmetic and copies ran while one was open for 8% -> 6% of each run, Pallas kernels for 50% -> 58%
where the time goes in v1:
time: 408 us; the launch traced here: 406 us
  Pallas kernels  240 us (59%)
  waiting for transfers between devices  68 us (17%)
  starting transfers between devices  39 us (10%)
  local copies, waits for them, and re-layouts  24.6 us (6%)
  other arithmetic  18 us (4%)
  between operations  15.6 us (4%)
    pallas_call x2, Pallas kernels, attend_back(): pl.pallas_call(functools.partial(attend_back_kernel, bq, bk, heads), grid...  96.1 us
    pallas_call x2, Pallas kernels, attend(): pl.pallas_call(functools.partial(attend_kernel, m, bq, bk, heads), grid_s...  59.6 us
    pallas_call x2, Pallas kernels, feed(): pl.pallas_call(functools.partial(feed_kernel, 4, add), grid=(2 * steps,),...  44 us
    ppermute x16, waiting for transfers between devices, swap_dp(): return lax.ppermute(value, 'dp', [(i, i ^ 1 << bit) for i in range(count)])  31.1 us
    ppermute x16, starting transfers between devices, swap_dp(): return lax.ppermute(value, 'dp', [(i, i ^ 1 << bit) for i in range(count)])  19.4 us
    unnamed x153, local copies, waits for them, and re-layouts  18.4 us
    pallas_call x6, Pallas kernels, by_rows(): pl.pallas_call(functools.partial(kernel, m), grid=(rows // step,), in_spe...  16 us
    ppermute x12, starting transfers between devices, swap_far(): return lax.ppermute(value, 'tensor', [(i, i ^ 2) for i in range(4)])  15.9 us
  transfers between devices with their start and end apart: 50, of which 25 were waited for; matrix products, arithmetic and copies ran while one was open for 6% of the time, Pallas kernels for 58%

profile of v1, /device:TPU:0, one launch (start us, length us, event | category | flops | bytes accessed | tf_op | source)
XLA Modules:
  0.0 406.0 jit_solution(8912608177037297415)
XLA Ops:
  8.6 3.0 collective-permute-start.5
  11.6 1.6 collective-permute-start
  13.2 2.6 collective-permute-start.1
  16.7 1.8 fusion.5
  20.6 1.5 collective-permute-done.1
  24.4 5.1 %collective-permute-done.2 = f32[2,2]{1,0:T(2,128)S(1)} collective-permute-done((f32[2,2]{1,0:T(2,128)S(1)}, f32[2,2]{1,0:T(2,128)S(1)}, u32[]{:S(2)}, u32[]{:S(2)}) %collective-permute-start.2) | collective-permute-done | bytes 48 | tf_op jit(solution)/shard_map/ppermute | solution.py:42
  29.7 3.1 collective-permute-start.4
  32.8 1.6 collective-permute-done.4
  35.3 2.0 mod_terms.1
  39.5 1.6 collective-permute-start.9
  41.0 4.2 %collective-permute-done.6 = f32[2,2,2,4608]{3,2,0,1:T(2,128)S(1)} collective-permute-done((f32[2,2,2,4608]{3,2,0,1:T(2,128)S(1)}, f32[2,2,2,4608]{3,2,0,1:T(2,128)S(1)}, u32[]{:S(2)}, u32[]{:S(2)}) %collective-permute-start.6) | collective-permute-done | bytes 147488 | tf_op jit(solution)/shard_map/ppermute | solution.py:42
  45.4 1.8 collective-permute-start.7
  47.2 6.2 %collective-permute-done.9 = bf16[2,2,96,576]{3,2,0,1:T(8,128)(2,1)S(1)} collective-permute-done((bf16[2,2,96,576]{3,2,0,1:T(8,128)(2,1)S(1)}, bf16[2,2,96,576]{3,2,0,1:T(8,128)(2,1)S(1)}, u32[]{:S(2)}, u32[]{:S(2)}) %collective-permute-start.9) | collective-permute-done | bytes 442400 | tf_op jit(solution)/shard_map/ppermute | solution.py:42
  53.6 2.7 collective-permute-start.8
  56.6 2.0 collective-permute-done.8
  59.4 3.4 collective-permute-done.11
  65.0 30.2 %attend.2 = (bf16[2048,768]{1,0:T(8,128)(2,1)}, bf16[576,2048]{1,0:T(8,128)(2,1)S(1)}, bf16[192,1024]{1,0:T(8,128)(2,1)S(1)}, bf16[192,1024]{1,0:T(8,128)(2,1)S(1)}, f32[3,1,2048]{2,1,0:T(1,128)S(1)}) custom-call(s32[4]{0:T(128)S(1)} %get-tuple-element.241.lo_ref, s32[4]{0:T(128)S(1)} %get-tuple-element.240.hi_ref, s32[1]{0:T(128)} %bitcast.28.place_ref, ...), custom_call_target="tpu_custom_call" | custom-call | flops 30198988800 | bytes 12582912 | tf_op jit(solution)/shard_map/attend/pallas_call | solution.py:362
  97.5 1.5 collective-permute-start.17
  99.7 29.4 %attend.3 = (bf16[2048,768]{1,0:T(8,128)(2,1)}, bf16[576,2048]{1,0:T(8,128)(2,1)S(1)}, bf16[192,1024]{1,0:T(8,128)(2,1)S(1)}, bf16[192,1024]{1,0:T(8,128)(2,1)S(1)}, f32[3,1,2048]{2,1,0:T(1,128)S(1)}) custom-call(s32[4]{0:T(128)S(1)} %get-tuple-element.239.lo_ref, s32[4]{0:T(128)S(1)} %get-tuple-element.238.hi_ref, s32[1]{0:T(128)} %bitcast.28.place_ref, ...), custom_call_target="tpu_custom_call" | custom-call | flops 30198988800 | bytes 12582912 | tf_op jit(solution)/shard_map/attend/pallas_call | solution.py:362
  130.7 1.5 copy-done.47
  132.9 9.1 %all-gather.3.cloned.1.call-done = bf16[1536,1728]{1,0:T(8,128)(2,1)} async-done(((bf16[96,1728]{1,0:T(8,128)(2,1)}), bf16[1536,1728]{1,0:T(8,128)(2,1)}) %all-gather.3.cloned.1.call-update) | async-done | bytes 5308432 | tf_op jit(solution)/shard_map/all_gather | solution.py:856
  145.4 2.3 collective-permute-done.18.arr_ref
  152.2 21.9 %feed.2 = (f32[512,768]{1,0:T(8,128)S(1)}, bf16[512,768]{1,0:T(8,128)(2,1)S(1)}, f32[512,768]{1,0:T(8,128)S(1)}, bf16[512,768]{1,0:T(8,128)(2,1)S(1)}, f32[768,3072]{1,0:T(8,128)}) custom-call(bf16[512,768]{1,0:T(8,128)(2,1)S(1)} %get-tuple-element.122.n0, bf16[512,768]{1,0:T(8,128)(2,1)S(1)} %collective-permute-done.19.n1, ...), custom_call_target="tpu_custom_call" | custom-call | flops 14495514624 | bytes 14155776 | tf_op jit(solution)/shard_map/feed/pallas_call | solution.py:540
  177.6 2.6 after_feed.2
  182.5 1.9 out_back.2
  186.2 1.5 collective-permute-start.28
  188.4 22.1 %feed.3 = (f32[512,768]{1,0:T(8,128)S(1)}, bf16[512,768]{1,0:T(8,128)(2,1)S(1)}, f32[512,768]{1,0:T(8,128)S(1)}, bf16[512,768]{1,0:T(8,128)(2,1)S(1)}, bf16[768,3072]{1,0:T(8,128)(2,1)}) custom-call(bf16[512,768]{1,0:T(8,128)(2,1)S(1)} %get-tuple-element.141.n0, bf16[512,768]{1,0:T(8,128)(2,1)S(1)} %collective-permute-done.26.n1, ...), custom_call_target="tpu_custom_call" | custom-call | flops 14495514624 | bytes 14155776 | tf_op jit(solution)/shard_map/feed/pallas_call | solution.py:540
  211.1 1.8 collective-permute-done.29.b1_ref
  214.0 3.0 after_feed.3
  218.4 2.3 collective-permute-done.31.g1_ref
  225.0 4.0 out_back.3
  229.7 1.6 collective-permute-start.34
  231.8 47.9 %attend_back.2 = (f32[2,512,768]{2,1,0:T(8,128)}, bf16[2,512,768]{2,1,0:T(8,128)(2,1)}, bf16[576,2048]{1,0:T(8,128)(2,1)}, f32[2,768]{1,0:T(2,128)S(1)}) custom-call(s32[8]{0:T(128)S(1)} %get-tuple-element.277.lo_ref, s32[8]{0:T(128)S(1)} %get-tuple-element.276.hi_ref, s32[1]{0:T(128)} %bitcast.28.place_ref, bf16[576,2048]{1,0:T(8,128)(2,1)} %copy-done.48, ...), custom_call_target="tpu_custom_call" | custom-call | flops 45298483200 | bytes 12582912 | tf_op jit(solution)/shard_map/attend_back/pallas_call | solution.py:418
  280.7 6.6 %project_grad.2.rest_0_ = f32[768,576]{1,0:T(8,128)} custom-call(bf16[2048,768]{1,0:T(8,128)(2,1)} %get-tuple-element.171.normed_ref, bf16[576,2048]{1,0:T(8,128)(2,1)} %get-tuple-element.172.back_ref), custom_call_target="tpu_custom_call" | custom-call | flops 36238786560 | bytes 6291456 | tf_op jit(solution)/shard_map/project_grad/pallas_call | solution.py:333
  287.4 2.3 fusion
  289.7 1.7 collective-permute-start.35
  291.4 48.2 %attend_back.3 = (f32[2,512,768]{2,1,0:T(8,128)}, bf16[2,512,768]{2,1,0:T(8,128)(2,1)}, bf16[576,2048]{1,0:T(8,128)(2,1)}, f32[2,768]{1,0:T(2,128)S(1)}) custom-call(s32[8]{0:T(128)S(1)} %get-tuple-element.275.lo_ref, s32[8]{0:T(128)S(1)} %get-tuple-element.274.hi_ref, s32[1]{0:T(128)} %bitcast.28.place_ref, bf16[576,2048]{1,0:T(8,128)(2,1)} %copy-done.47, ...), custom_call_target="tpu_custom_call" | custom-call | flops 45298483200 | bytes 12582912 | tf_op jit(solution)/shard_map/attend_back/pallas_call | solution.py:418
  341.5 7.4 %project_grad.3 = f32[768,576]{1,0:T(8,128)} custom-call(bf16[2048,768]{1,0:T(8,128)(2,1)} %get-tuple-element.187.normed_ref, bf16[576,2048]{1,0:T(8,128)(2,1)} %get-tuple-element.188.back_ref, f32[768,576]{1,0:T(8,128)} %project_grad.2.rest_0_), custom_call_target="tpu_custom_call" | custom-call | flops 36238786560 | bytes 6291456 | tf_op jit(solution)/shard_map/project_grad/pallas_call | solution.py:333
  348.9 2.3 fusion.1
  352.3 1.5 collective-permute-start.38
  354.8 2.0 collective-permute-start.39
  356.8 4.3 %finish.2.rest_0_ = f32[2,512,768]{2,1,0:T(8,128)} custom-call(f32[2,4608]{1,0:T(2,128)} %copy-done.2, bf16[2,512,768]{2,1,0:T(8,128)(2,1)} %tok_ref.11, f32[2,512,768]{2,1,0:T(8,128)} %get-tuple-element.169.keep_ref, bf16[2,512,768]{2,1,0:T(8,128)(2,1)} %copy-done.54, bf16[512,768]{1,0:T(8,128)(2,1)} %copy-done.57, f32[512,768]{1,0:T(8,128)} %copy-done.3), custom_call_target="tpu_custom_call" | custom-call | flops 15728640 | bytes 12582912 | tf_op jit(solution)/shard_map/finish/pallas_call | solution.py:740
  361.2 11.4 %collective-permute-done.38.crossed_ref = bf16[512,768]{1,0:T(8,128)(2,1)S(1)} collective-permute-done((bf16[512,768]{1,0:T(8,128)(2,1)}, bf16[512,768]{1,0:T(8,128)(2,1)S(1)}, u32[]{:S(2)}, u32[]{:S(2)}) %collective-permute-start.38) | collective-permute-done | bytes 786464 | tf_op jit(solution)/shard_map/ppermute | solution.py:33
  374.3 2.6 collective-permute-done.46
  377.3 4.2 %finish.3 = f32[2,512,768]{2,1,0:T(8,128)} custom-call(f32[2,4608]{1,0:T(2,128)} %copy-done.2, bf16[2,512,768]{2,1,0:T(8,128)(2,1)} %tok_ref.11, f32[2,512,768]{2,1,0:T(8,128)} %get-tuple-element.183.keep_ref, bf16[2,512,768]{2,1,0:T(8,128)(2,1)} %collective-permute-done.37.arr_ref, bf16[512,768]{1,0:T(8,128)(2,1)} %copy-done.56, ...), custom_call_target="tpu_custom_call", output_to_operand_aliasing={{}: (6, {})} | custom-call | flops 15728640 | bytes 12582912 | tf_op jit(solution)/shard_map/finish/pallas_call | solution.py:740
  381.5 3.7 collective-permute-done.47
  390.2 1.5 collective-permute-start.42
  391.7 3.7 collective-permute-done.41
  (315 shorter events, 58.3 us)
Async XLA Ops:
  7.2 134.8 %all-gather.3.cloned.1.call-start = ((), (), s32[]{:S(2)}) async-start(), calls=%async_computation.2 | async-start | bytes 5849088 | tf_op jit(solution)/shard_map/all_gather | solution.py:856
  8.6 26.0 %collective-permute-start.5 = (bf16[512,768]{1,0:T(8,128)(2,1)S(1)}, bf16[512,768]{1,0:T(8,128)(2,1)S(1)}, u32[]{:S(2)}, u32[]{:S(2)}) collective-permute-start(bf16[512,768]{1,0:T(8,128)(2,1)S(1)} %slice_bitcast_fusion.3.t0), channel_id=1, source_target_pairs={{0,2},{1,3},{2,0},{3,1},{4,6},{5,7},{6,4},{7,5},{8,10},{9,11},{10,... | collective-permute-start | bytes 2359304 | tf_op jit(solution)/shard_map/ppermute | solution.py:33
  11.6 53.4 %collective-permute-start.15 = (bf16[512,768]{1,0:T(8,128)(2,1)S(1)}, bf16[512,768]{1,0:T(8,128)(2,1)}, u32[]{:S(2)}, u32[]{:S(2)}) collective-permute-start(bf16[512,768]{1,0:T(8,128)(2,1)S(1)} %slice_bitcast_fusion.3.t0), channel_id=1, source_target_pairs={{0,1},{1,0},{2,3},{3,2},{4,5},{5,4},{6,7},{7,6},{8,9},{9,8},{10,11... | collective-permute-start | bytes 2359304 | tf_op jit(solution)/shard_map/ppermute | solution.py:37
  11.6 11.3 %collective-permute-start = (f32[2]{0:T(128)S(1)}, f32[2]{0:T(128)S(1)}, u32[]{:S(2)}, u32[]{:S(2)}) collective-permute-start(f32[2]{0:T(128)S(1)} %get-tuple-element.273), channel_id=1, source_target_pairs={{0,4},{4,0},{8,12},{12,8},{16,20},{20,16},{24,28},{28,24},{1,5},{5... | collective-permute-start | bytes 32 | tf_op jit(solution)/shard_map/ppermute | solution.py:42
  13.2 8.9 %collective-permute-start.1 = (bf16[96,576]{1,0:T(8,128)(2,1)S(1)}, bf16[96,576]{1,0:T(8,128)(2,1)S(1)}, u32[]{:S(2)}, u32[]{:S(2)}) collective-permute-start(bf16[96,576]{1,0:T(8,128)(2,1)S(1)} %copy-done.60), channel_id=1, source_target_pairs={{0,16},{4,20},{8,24},{12,28},{16,0},{20,4},{24,8},{28,12},{1,17},{... | collective-permute-start | bytes 331784 | tf_op jit(solution)/shard_map/ppermute | solution.py:42
  22.2 7.3 %collective-permute-start.3 = (bf16[2,96,576]{2,1,0:T(8,128)(2,1)S(1)}, bf16[2,96,576]{2,1,0:T(8,128)(2,1)S(1)}, u32[]{:S(2)}, u32[]{:S(2)}) collective-permute-start(bf16[2,96,576]{2,1,0:T(8,128)(2,1)S(1)} %pad_maximum_fusion.6), channel_id=1, source_target_pairs={{0,8},{4,12},{8,0},{12,4},{16,24},{20,28},{24,16},{28,20},{1,9},{5... | collective-permute-start | bytes 663560 | tf_op jit(solution)/shard_map/ppermute | solution.py:42
  23.0 6.6 %collective-permute-start.2 = (f32[2,2]{1,0:T(2,128)S(1)}, f32[2,2]{1,0:T(2,128)S(1)}, u32[]{:S(2)}, u32[]{:S(2)}) collective-permute-start(f32[2,2]{1,0:T(2,128)S(1)} %pad_maximum_fusion.14), channel_id=1, source_target_pairs={{0,8},{4,12},{8,0},{12,4},{16,24},{20,28},{24,16},{28,20},{1,9},{5... | collective-permute-start | bytes 56 | tf_op jit(solution)/shard_map/ppermute | solution.py:42
  29.7 4.7 %collective-permute-start.4 = (f32[2,2,2]{2,1,0:T(2,128)S(1)}, f32[2,2,2]{2,1,0:T(2,128)S(1)}, u32[]{:S(2)}, u32[]{:S(2)}) collective-permute-start(f32[2,2,2]{2,1,0:T(2,128)S(1)} %pad_maximum_fusion.13), channel_id=1, source_target_pairs={{0,16},{4,20},{8,24},{12,28},{16,0},{20,4},{24,8},{28,12},{1,17},{... | collective-permute-start | bytes 104 | tf_op jit(solution)/shard_map/ppermute | solution.py:42
  38.4 6.9 %collective-permute-start.6 = (f32[2,2,2,4608]{3,2,0,1:T(2,128)S(1)}, f32[2,2,2,4608]{3,2,0,1:T(2,128)S(1)}, u32[]{:S(2)}, u32[]{:S(2)}) collective-permute-start(f32[2,2,2,4608]{3,2,0,1:T(2,128)S(1)} %bitcast.151), channel_id=1, source_target_pairs={{0,4},{4,0},{8,12},{12,8},{16,20},{20,16},{24,28},{28,24},{1,5},{5... | collective-permute-start | bytes 442376 | tf_op jit(solution)/shard_map/ppermute | solution.py:42
  39.5 13.9 %collective-permute-start.9 = (bf16[2,2,96,576]{3,2,0,1:T(8,128)(2,1)S(1)}, bf16[2,2,96,576]{3,2,0,1:T(8,128)(2,1)S(1)}, u32[]{:S(2)}, u32[]{:S(2)}) collective-permute-start(bf16[2,2,96,576]{3,2,0,1:T(8,128)(2,1)S(1)} %pad_maximum_fusion.2), channel_id=1, source_target_pairs={{0,4},{4,0},{8,12},{12,8},{16,20},{20,16},{24,28},{28,24},{1,5},{5... | collective-permute-start | bytes 1327112 | tf_op jit(solution)/shard_map/ppermute | solution.py:42
  45.4 8.2 %collective-permute-start.7 = (f32[2,2,4608]{2,1,0:T(2,128)S(1)}, f32[2,2,4608]{2,1,0:T(2,128)S(1)}, u32[]{:S(2)}, u32[]{:S(2)}) collective-permute-start(f32[2,2,4608]{2,1,0:T(2,128)S(1)} %slice_bitcast_fusion.7), channel_id=1, source_target_pairs={{0,8},{4,12},{8,0},{12,4},{16,24},{20,28},{24,16},{28,20},{1,9},{5... | collective-permute-start | bytes 221192 | tf_op jit(solution)/shard_map/ppermute | solution.py:42
  53.5 335.6 %reduce-scatter.2.cloned.1.call-start = ((), (), s32[]{:S(2)}) async-start(), calls=%async_computation.1 | async-start | bytes 5308416 | tf_op jit(solution)/shard_map/reduce_scatter | solution.py:947
  53.6 4.9 %collective-permute-start.8 = (f32[2,4608]{1,0:T(2,128)S(1)}, f32[2,4608]{1,0:T(2,128)S(1)}, u32[]{:S(2)}, u32[]{:S(2)}) collective-permute-start(f32[2,4608]{1,0:T(2,128)S(1)} %slice_bitcast_fusion.9), channel_id=1, source_target_pairs={{0,16},{4,20},{8,24},{12,28},{16,0},{20,4},{24,8},{28,12},{1,17},{... | collective-permute-start | bytes 110600 | tf_op jit(solution)/shard_map/ppermute | solution.py:42
  56.5 2.4 collective-permute-start.10
  58.9 4.0 collective-permute-start.11
  64.2 34.8 %collective-permute-start.13 = (bf16[512,768]{1,0:T(8,128)(2,1)S(1)}, bf16[512,768]{1,0:T(8,128)(2,1)S(1)}, u32[]{:S(2)}, u32[]{:S(2)}) collective-permute-start(bf16[512,768]{1,0:T(8,128)(2,1)S(1)} %slice_bitcast_fusion.2.t0), channel_id=1, source_target_pairs={{0,1},{1,0},{2,3},{3,2},{4,5},{5,4},{6,7},{7,6},{8,9},{9,8},{10,11... | collective-permute-start | bytes 2359304 | tf_op jit(solution)/shard_map/ppermute | solution.py:37
  64.5 32.9 %collective-permute-start.14 = (bf16[512,768]{1,0:T(8,128)(2,1)S(1)}, bf16[512,768]{1,0:T(8,128)(2,1)S(1)}, u32[]{:S(2)}, u32[]{:S(2)}) collective-permute-start(bf16[512,768]{1,0:T(8,128)(2,1)S(1)} %slice_bitcast_fusion.2.t0), channel_id=1, source_target_pairs={{0,2},{1,3},{2,0},{3,1},{4,6},{5,7},{6,4},{7,5},{8,10},{9,11},{10,... | collective-permute-start | bytes 2359304 | tf_op jit(solution)/shard_map/ppermute | solution.py:33
  97.4 2.3 collective-permute-start.16
  97.5 34.7 %collective-permute-start.17 = (bf16[192,1024]{1,0:T(8,128)(2,1)S(1)}, bf16[192,1024]{1,0:T(8,128)(2,1)S(1)}, u32[]{:S(2)}, u32[]{:S(2)}) collective-permute-start(bf16[192,1024]{1,0:T(8,128)(2,1)S(1)} %get-tuple-element.117.far_ref), channel_id=1, source_target_pairs={{0,2},{1,3},{2,0},{3,1},{4,6},{5,7},{6,4},{7,5},{8,10},{9,11},{10,... | collective-permute-start | bytes 1179656 | tf_op jit(solution)/shard_map/ppermute | solution.py:33
  145.3 2.4 collective-permute-start.18
  148.7 2.4 collective-permute-start.19
  148.9 3.3 collective-permute-start.20
  149.3 24.8 %collective-permute-start.21 = (bf16[192,1024]{1,0:T(8,128)(2,1)S(1)}, bf16[192,1024]{1,0:T(8,128)(2,1)S(1)}, u32[]{:S(2)}, u32[]{:S(2)}) collective-permute-start(bf16[192,1024]{1,0:T(8,128)(2,1)S(1)} %copy-done.20), channel_id=1, source_target_pairs={{0,2},{1,3},{2,0},{3,1},{4,6},{5,7},{6,4},{7,5},{8,10},{9,11},{10,... | collective-permute-start | bytes 1179656 | tf_op jit(solution)/shard_map/ppermute | solution.py:33
  174.1 2.9 collective-permute-start.23
  174.3 3.3 collective-permute-start.24
  176.7 3.6 collective-permute-start.22
  180.2 2.3 collective-permute-start.25
  181.4 6.3 %collective-permute-start.27 = (bf16[512,768]{1,0:T(8,128)(2,1)S(1)}, bf16[512,768]{1,0:T(8,128)(2,1)S(1)}, u32[]{:S(2)}, u32[]{:S(2)}) collective-permute-start(bf16[512,768]{1,0:T(8,128)(2,1)S(1)} %get-tuple-element.142.g0), channel_id=1, source_target_pairs={{0,1},{1,0},{2,3},{3,2},{4,5},{5,4},{6,7},{7,6},{8,9},{9,8},{10,11... | collective-permute-start | bytes 2359304 | tf_op jit(solution)/shard_map/ppermute | solution.py:37
  186.2 24.3 %collective-permute-start.28 = (bf16[192,1024]{1,0:T(8,128)(2,1)S(1)}, bf16[192,1024]{1,0:T(8,128)(2,1)S(1)}, u32[]{:S(2)}, u32[]{:S(2)}) collective-permute-start(bf16[192,1024]{1,0:T(8,128)(2,1)S(1)} %get-tuple-element.140), channel_id=1, source_target_pairs={{0,2},{1,3},{2,0},{3,1},{4,6},{5,7},{6,4},{7,5},{8,10},{9,11},{10,... | collective-permute-start | bytes 1179656 | tf_op jit(solution)/shard_map/ppermute | solution.py:33
  210.5 2.4 collective-permute-start.29
  210.7 3.3 collective-permute-start.30
  218.2 2.5 collective-permute-start.31
  229.7 57.7 %collective-permute-start.34 = (bf16[192,1024]{1,0:T(8,128)(2,1)}, bf16[192,1024]{1,0:T(8,128)(2,1)S(1)}, u32[]{:S(2)}, u32[]{:S(2)}) collective-permute-start(bf16[192,1024]{1,0:T(8,128)(2,1)} %get-tuple-element.161), channel_id=1, source_target_pairs={{0,2},{1,3},{2,0},{3,1},{4,6},{5,7},{6,4},{7,5},{8,10},{9,11},{10,... | collective-permute-start | bytes 1179656 | tf_op jit(solution)/shard_map/ppermute | solution.py:33
  231.3 48.4 %collective-permute-start.32 = (bf16[768,192]{1,0:T(8,128)(2,1)S(1)}, bf16[768,192]{1,0:T(8,128)(2,1)S(1)}, u32[]{:S(2)}, u32[]{:S(2)}) collective-permute-start(bf16[768,192]{1,0:T(8,128)(2,1)S(1)} %get-tuple-element.168), channel_id=1, source_target_pairs={{0,2},{1,3},{2,0},{3,1},{4,6},{5,7},{6,4},{7,5},{8,10},{9,11},{10,... | collective-permute-start | bytes 884744 | tf_op jit(solution)/shard_map/ppermute | solution.py:33
  279.7 7.7 %collective-permute-start.33 = (bf16[2,512,768]{2,1,0:T(8,128)(2,1)}, bf16[2,512,768]{2,1,0:T(8,128)(2,1)S(1)}, u32[]{:S(2)}, u32[]{:S(2)}) collective-permute-start(bf16[2,512,768]{2,1,0:T(8,128)(2,1)} %get-tuple-element.170), channel_id=1, source_target_pairs={{0,1},{1,0},{2,3},{3,2},{4,5},{5,4},{6,7},{7,6},{8,9},{9,8},{10,11... | collective-permute-start | bytes 4718600 | tf_op jit(solution)/shard_map/ppermute | solution.py:37
  280.7 58.9 %collective-permute-start.36 = (bf16[2,2,96,192]{3,2,1,0:T(8,128)(2,1)}, bf16[2,2,96,192]{3,2,1,0:T(8,128)(2,1)}, u32[]{:S(2)}, u32[]{:S(2)}) collective-permute-start(bf16[2,2,96,192]{3,2,1,0:T(8,128)(2,1)} %fusion.7), channel_id=1, source_target_pairs={{0,4},{4,0},{8,12},{12,8},{16,20},{20,16},{24,28},{28,24},{1,5},{5... | collective-permute-start | bytes 442376 | tf_op jit(solution)/shard_map/ppermute | solution.py:42
  289.7 49.9 %collective-permute-start.35 = (bf16[512,768]{1,0:T(8,128)(2,1)S(1)}, bf16[512,768]{1,0:T(8,128)(2,1)S(1)}, u32[]{:S(2)}, u32[]{:S(2)}) collective-permute-start(bf16[512,768]{1,0:T(8,128)(2,1)S(1)} %fusion), channel_id=1, source_target_pairs={{0,2},{1,3},{2,0},{3,1},{4,6},{5,7},{6,4},{7,5},{8,10},{9,11},{10,... | collective-permute-start | bytes 2359304 | tf_op jit(solution)/shard_map/ppermute | solution.py:33
  340.5 8.4 %collective-permute-start.37 = (bf16[2,512,768]{2,1,0:T(8,128)(2,1)}, bf16[2,512,768]{2,1,0:T(8,128)(2,1)}, u32[]{:S(2)}, u32[]{:S(2)}) collective-permute-start(bf16[2,512,768]{2,1,0:T(8,128)(2,1)} %get-tuple-element.184), channel_id=1, source_target_pairs={{0,1},{1,0},{2,3},{3,2},{4,5},{5,4},{6,7},{7,6},{8,9},{9,8},{10,11... | collective-permute-start | bytes 4718600 | tf_op jit(solution)/shard_map/ppermute | solution.py:37
  340.8 8.0 %collective-permute-start.43 = (f32[2,4608]{1,0:T(2,128)S(1)}, f32[2,4608]{1,0:T(2,128)S(1)}, u32[]{:S(2)}, u32[]{:S(2)}) collective-permute-start(f32[2,4608]{1,0:T(2,128)S(1)} %pad_maximum_fusion.9), channel_id=1, source_target_pairs={{0,2},{1,3},{2,0},{3,1},{4,6},{5,7},{6,4},{7,5},{8,10},{9,11},{10,... | collective-permute-start | bytes 110600 | tf_op jit(solution)/shard_map/ppermute | solution.py:33
  351.3 2.5 collective-permute-start.44
  352.3 20.2 %collective-permute-start.38 = (bf16[512,768]{1,0:T(8,128)(2,1)}, bf16[512,768]{1,0:T(8,128)(2,1)S(1)}, u32[]{:S(2)}, u32[]{:S(2)}) collective-permute-start(bf16[512,768]{1,0:T(8,128)(2,1)} %fusion.1), channel_id=1, source_target_pairs={{0,2},{1,3},{2,0},{3,1},{4,6},{5,7},{6,4},{7,5},{8,10},{9,11},{10,... | collective-permute-start | bytes 2359304 | tf_op jit(solution)/shard_map/ppermute | solution.py:33
  353.8 7.3 %collective-permute-start.45 = (f32[2,4608]{1,0:T(2,128)S(1)}, f32[2,4608]{1,0:T(2,128)S(1)}, u32[]{:S(2)}, u32[]{:S(2)}) collective-permute-start(f32[2,4608]{1,0:T(2,128)S(1)} %add.94), channel_id=1, source_target_pairs={{0,4},{4,0},{8,12},{12,8},{16,20},{20,16},{24,28},{28,24},{1,5},{5... | collective-permute-start | bytes 110600 | tf_op jit(solution)/shard_map/ppermute | solution.py:42
  354.8 17.7 %collective-permute-start.39 = (bf16[2,2,96,576]{3,2,1,0:T(8,128)(2,1)}, bf16[2,2,96,576]{3,2,1,0:T(8,128)(2,1)}, u32[]{:S(2)}, u32[]{:S(2)}) collective-permute-start(bf16[2,2,96,576]{3,2,1,0:T(8,128)(2,1)} %fusion.3), channel_id=1, source_target_pairs={{0,4},{4,0},{8,12},{12,8},{16,20},{20,16},{24,28},{28,24},{1,5},{5... | collective-permute-start | bytes 1327112 | tf_op jit(solution)/shard_map/ppermute | solution.py:42
  372.5 4.4 %collective-permute-start.46 = (f32[2,2,4608]{2,1,0:T(2,128)S(1)}, f32[2,2,4608]{2,1,0:T(2,128)S(1)}, u32[]{:S(2)}, u32[]{:S(2)}) collective-permute-start(f32[2,2,4608]{2,1,0:T(2,128)S(1)} %pad_maximum_fusion.8), channel_id=1, source_target_pairs={{0,8},{4,12},{8,0},{12,4},{16,24},{20,28},{24,16},{28,20},{1,9},{5... | collective-permute-start | bytes 221192 | tf_op jit(solution)/shard_map/ppermute | solution.py:42
  377.0 8.2 %collective-permute-start.47 = (f32[2,2,2,4608]{3,2,1,0:T(2,128)S(1)}, f32[2,2,2,4608]{3,2,1,0:T(2,128)S(1)}, u32[]{:S(2)}, u32[]{:S(2)}) collective-permute-start(f32[2,2,2,4608]{3,2,1,0:T(2,128)S(1)} %get-tuple-element.257), channel_id=1, source_target_pairs={{0,16},{4,20},{8,24},{12,28},{16,0},{20,4},{24,8},{28,12},{1,17},{... | collective-permute-start | bytes 442376 | tf_op jit(solution)/shard_map/ppermute | solution.py:42
  377.1 10.7 %collective-permute-start.40 = (bf16[2,96,768]{2,1,0:T(8,128)(2,1)S(1)}, bf16[2,96,768]{2,1,0:T(8,128)(2,1)S(1)}, u32[]{:S(2)}, u32[]{:S(2)}) collective-permute-start(bf16[2,96,768]{2,1,0:T(8,128)(2,1)S(1)} %fusion.4), channel_id=1, source_target_pairs={{0,8},{4,12},{8,0},{12,4},{16,24},{20,28},{24,16},{28,20},{1,9},{5... | collective-permute-start | bytes 884744 | tf_op jit(solution)/shard_map/ppermute | solution.py:42
  388.0 7.5 %collective-permute-start.41 = (bf16[96,768]{1,0:T(8,128)(2,1)S(1)}, bf16[96,768]{1,0:T(8,128)(2,1)S(1)}, u32[]{:S(2)}, u32[]{:S(2)}) collective-permute-start(bf16[96,768]{1,0:T(8,128)(2,1)S(1)} %fusion.8), channel_id=1, source_target_pairs={{0,16},{4,20},{8,24},{12,28},{16,0},{20,4},{24,8},{28,12},{1,17},{... | collective-permute-start | bytes 442376 | tf_op jit(solution)/shard_map/ppermute | solution.py:42
  390.2 6.8 %collective-permute-start.42 = (bf16[96,1536]{1,0:T(8,128)(2,1)S(1)}, bf16[96,1536]{1,0:T(8,128)(2,1)S(1)}, u32[]{:S(2)}, u32[]{:S(2)}) collective-permute-start(bf16[96,1536]{1,0:T(8,128)(2,1)S(1)} %broadcast_select_fusion), channel_id=1, source_target_pairs={{0,2},{1,3},{2,0},{3,1},{4,6},{5,7},{6,4},{7,5},{8,10},{9,11},{10,... | collective-permute-start | bytes 884744 | tf_op jit(solution)/shard_map/ppermute | solution.py:33
  (73 other events, 703.8 us)
Sparse Core Ops, SparseCore 0:
  53.6 88.3 all-gather.2
  218.5 98.5 reduce-scatter.1

commit v2 on v1

--- a/solution.py
+++ b/solution.py
@@ -37,9 +37,12 @@
     return lax.ppermute(value, "tensor", [(i, i ^ 1) for i in range(4)])
 
 
+def swap_by(value, mask):
+    return lax.ppermute(value, "dp", [(i, i ^ mask) for i in range(lax.axis_size("dp"))])
+
+
 def swap_dp(value, bit):
-    count = lax.axis_size("dp")
-    return lax.ppermute(value, "dp", [(i, i ^ (1 << bit)) for i in range(count)])
+    return swap_by(value, 1 << bit)
 
 
 def after(value, other):
@@ -75,8 +78,13 @@
 
 def gather_relative(value, first=lambda value, bit: value):
     current = value
-    for bit in range(dp_bits()):
+    count = dp_bits()
+    for bit in range(count):
         current = first(current, bit)
+        if bit == 1 and count == 3:
+            others = [swap_by(current, k << 1) for k in range(1, 4)]
+            current = jnp.stack([current, *others])
+            break
         current = jnp.stack([current, swap_dp(current, bit)])
     return current.reshape((-1,) + value.shape)
 
@@ -86,6 +94,9 @@
     current = terms.reshape((2,) * count + terms.shape[1:])
     for bit in range(count):
         current = first(current, bit)
+        if bit == 1 and count == 3:
+            current = current.reshape((4,) + current.shape[2:])
+            return current[0] + sum(swap_by(current[k], k << 1) for k in range(1, 4))
         place = count - 1 - bit
         kept = lax.index_in_dim(current, 0, place, keepdims=False)
         sent = lax.index_in_dim(current, 1, place, keepdims=False)
@@ -399,7 +410,7 @@
             jax.ShapeDtypeStruct((heads, 1, length), F32),
         ],
         cost_estimate=pl.CostEstimate(
-            flops=heads * length * length * 2400,
+            flops=heads * length * length * 800,
             bytes_accessed=length * width * 8,
             transcendentals=heads * length * length // 2,
         ),
@@ -671,7 +682,7 @@
         cost_estimate=pl.CostEstimate(
             flops=16 * total * width * size, bytes_accessed=total * width * 4, transcendentals=0
         ),
-        compiler_params=pltpu.CompilerParams(vmem_limit_bytes=24 * 2**20),
+        compiler_params=None if last else pltpu.CompilerParams(vmem_limit_bytes=24 * 2**20),
         name="out_back",
     )(place, *grads, own, away, pack, *(before if add else ()))
 
@@ -817,12 +828,8 @@
     def with_stamps(value, bit):
         return advance(value, bit - 1) if bit >= 1 else value
 
-    begun = []
-
     def with_terms(value, bit):
-        if bit == 0:
-            begun.append(value)
-        return value
+        return advance(value, count - 2) if bit == 0 else value
 
     ready = tokens[0]
     across = swap_far(ready)
@@ -841,15 +848,15 @@
     bias = jnp.where(
         jnp.arange(slots)[:, None] == device, b_ada.astype(F32)[None, :], 0.0
     ).reshape(-1)
-    terms = mod_terms(advance(after(cond, across), count - 2), w_ada, bias)
+    terms = mod_terms(after(cond, across), w_ada, bias)
     mods = scatter_relative(terms.reshape(-1, micro_count, terms.shape[1]), with_terms)
 
-    mods = after(advance(mods, count - 1), (blocks[0][3], tables, doc_rows, bounds))
+    mods = after(mods, (blocks[0][3], tables, doc_rows, bounds))
+    mods = advance(mods + swap_far(mods), count - 1)
     wq = states[-1].reshape(width, -1)
-    mods = mods + swap_far(mods)
     mods = mods + swap_near(mods)
 
-    pack = after(pack, begun[0])
+    pack = after(pack, cond)
     groups = [
         [4 * i + 2 * j + c for i in range(lax.axis_size("dp")) for j in range(2)] for c in range(2)
     ]
@@ -1003,8 +1010,12 @@
     pieces = jnp.split(total, 2 * hid // CHUNK, axis=1)
     g_up = jnp.concatenate(pieces[0::2], axis=1)
     g_down = jnp.concatenate(pieces[1::2], axis=1).T
+    d_mods = jnp.stack(mod_grads)
+    d_mods = after(d_mods + swap_far(d_mods), g_last)
+    d_mods = d_mods + swap_near(d_mods)
+    all_mods = gather_relative(d_mods).reshape(-1, d_mods.shape[1])
     current, sent = halves(by_bits(g_last), 0, falling)
-    swapped = after(swap_dp(sent, 0), first_done)
+    swapped = after(swap_dp(sent, 0), (first_done, all_mods))
     current = jnp.concatenate(
         [out_keep + out_half.astype(F32), current + swapped.astype(F32)], axis=-1
     )
@@ -1016,12 +1027,6 @@
     g_out = current[:, :part].T
     g_qkv = current[:, part:]
 
-    d_mods = jnp.stack(mod_grads)
-    d_mods = after(d_mods + swap_far(d_mods), g_last)
-    d_mods = d_mods + swap_near(d_mods)
-    all_mods = gather_relative(
-        d_mods, lambda value, bit: after(value, swapped) if bit == 1 else value
-    ).reshape(-1, d_mods.shape[1])
     g_ada = lax.dot_general(
         cond.astype(F32),
         all_mods,

time: 408 us -> 391 us (0.958)
  Pallas kernels: 240 us -> 221 us
  waiting for transfers between devices: 68 us -> 50.7 us
  starting transfers between devices: 39 us -> 55.1 us
    ppermute x16 -> x19, starting transfers between devices: 19.4 us -> 34.5 us  [swap_by(): lax.ppermute(value, 'dp', [(i, i ^ mask) for i in range(lax.axis_size('dp...]
    pallas_call x2, Pallas kernels: 96.1 us -> 81 us  [attend_back(): pl.pallas_call(functools.partial(attend_back_kernel, bq, bk, heads), grid...]
    all_gather x1, waiting for transfers between devices: 9.09 us -> 0.01 us  [per_device(): pack = lax.all_gather(pack, ('dp', 'tensor'), axis_index_groups=groups)]
    ppermute x12, waiting for transfers between devices: 14.8 us -> 6.48 us  [swap_far(): return lax.ppermute(value, 'tensor', [(i, i ^ 2) for i in range(4)])]
    pallas_call x2, Pallas kernels: 59.6 us -> 53.8 us  [attend(): pl.pallas_call(functools.partial(attend_kernel, m, bq, bk, heads), grid_s...]
    unnamed x153 -> x148, local copies, waits for them, and re-layouts: 18.4 us -> 15.7 us
    ppermute x16 -> x19, waiting for transfers between devices: 31.1 us -> 32.8 us  [swap_by(): lax.ppermute(value, 'dp', [(i, i ^ mask) for i in range(lax.axis_size('dp...]
  transfers between devices with their start and end apart: 50 -> 53, of which waited for: 25 -> 24; matrix products, arithmetic and copies ran while one was open for 6% -> 6% of each run, Pallas kernels for 58% -> 56%
where the time goes in v2:
time: 391 us; the launch traced here: 385 us
  Pallas kernels  221 us (57%)
  starting transfers between devices  55.1 us (14%)
  waiting for transfers between devices  50.7 us (13%)
  local copies, waits for them, and re-layouts  21.9 us (6%)
  other arithmetic  20.1 us (5%)
  between operations  15.6 us (4%)
    pallas_call x2, Pallas kernels, attend_back(): pl.pallas_call(functools.partial(attend_back_kernel, bq, bk, heads), grid...  81 us
    pallas_call x2, Pallas kernels, attend(): pl.pallas_call(functools.partial(attend_kernel, m, bq, bk, heads), grid_s...  53.8 us
    pallas_call x2, Pallas kernels, feed(): pl.pallas_call(functools.partial(feed_kernel, 4, add), grid=(2 * steps,),...  44.4 us
    ppermute x19, starting transfers between devices, swap_by(): lax.ppermute(value, 'dp', [(i, i ^ mask) for i in range(lax.axis_size('dp...  34.5 us
    ppermute x19, waiting for transfers between devices, swap_by(): lax.ppermute(value, 'dp', [(i, i ^ mask) for i in range(lax.axis_size('dp...  32.8 us
    pallas_call x6, Pallas kernels, by_rows(): pl.pallas_call(functools.partial(kernel, m), grid=(rows // step,), in_spe...  15.9 us
    unnamed x148, local copies, waits for them, and re-layouts  15.7 us
    ppermute x12, starting transfers between devices, swap_far(): return lax.ppermute(value, 'tensor', [(i, i ^ 2) for i in range(4)])  15.7 us
  transfers between devices with their start and end apart: 53, of which 24 were waited for; matrix products, arithmetic and copies ran while one was open for 6% of the time, Pallas kernels for 56%

profile of v2, /device:TPU:0, one launch (start us, length us, event | category | flops | bytes accessed | tf_op | source)
XLA Modules:
  0.0 385.2 jit_solution(3248217287745716650)
XLA Ops:
  7.3 1.3 slice_bitcast_fusion.3.t0
  8.6 3.0 collective-permute-start.5
  11.6 1.6 collective-permute-start
  13.2 2.6 collective-permute-start.1
  17.1 5.0 %collective-permute-done.1 = bf16[96,576]{1,0:T(8,128)(2,1)S(1)} collective-permute-done((bf16[96,576]{1,0:T(8,128)(2,1)S(1)}, bf16[96,576]{1,0:T(8,128)(2,1)S(1)}, u32[]{:S(2)}, u32[]{:S(2)}) %collective-permute-start.1) | collective-permute-done | bytes 110624 | tf_op jit(solution)/shard_map/ppermute | solution.py:41
  22.2 3.6 collective-permute-start.4
  27.7 2.6 collective-permute-done.3
  31.9 1.8 fusion.5
  34.2 8.8 %collective-permute-done.6 = bf16[2,96,576]{2,1,0:T(8,128)(2,1)S(1)} collective-permute-done((bf16[2,96,576]{2,1,0:T(8,128)(2,1)S(1)}, bf16[2,96,576]{2,1,0:T(8,128)(2,1)S(1)}, u32[]{:S(2)}, u32[]{:S(2)}) %collective-permute-start.6) | collective-permute-done | bytes 221216 | tf_op jit(solution)/shard_map/ppermute | solution.py:41
  43.8 2.0 mod_terms.1
  47.4 2.1 collective-permute-start.13
  49.5 3.8 collective-permute-done.7
  54.4 3.4 collective-permute-start.9
  59.3 2.5 collective-permute-done.9
  62.2 4.5 %collective-permute-done.12 = f32[2,4608]{1,0:T(2,128)S(1)} collective-permute-done((f32[2,4608]{1,0:T(2,128)S(1)}, f32[2,4608]{1,0:T(2,128)S(1)}, u32[]{:S(2)}, u32[]{:S(2)}) %collective-permute-start.12) | collective-permute-done | bytes 36896 | tf_op jit(solution)/shard_map/ppermute | solution.py:33
  68.5 24.4 %attend.2 = (bf16[2048,768]{1,0:T(8,128)(2,1)}, bf16[576,2048]{1,0:T(8,128)(2,1)S(1)}, bf16[192,1024]{1,0:T(8,128)(2,1)S(1)}, bf16[192,1024]{1,0:T(8,128)(2,1)S(1)}, f32[3,1,2048]{2,1,0:T(1,128)S(1)}) custom-call(s32[4]{0:T(128)S(1)} %get-tuple-element.237.lo_ref, s32[4]{0:T(128)S(1)} %get-tuple-element.236.hi_ref, s32[1]{0:T(128)} %bitcast.29.place_ref, ...), custom_call_target="tpu_custom_call" | custom-call | flops 10066329600 | bytes 12582912 | tf_op jit(solution)/shard_map/attend/pallas_call | solution.py:373
  93.6 1.4 copy-done.45
  95.5 1.5 collective-permute-start.19
  97.4 29.4 %attend.3 = (bf16[2048,768]{1,0:T(8,128)(2,1)}, bf16[576,2048]{1,0:T(8,128)(2,1)S(1)}, bf16[192,1024]{1,0:T(8,128)(2,1)S(1)}, bf16[192,1024]{1,0:T(8,128)(2,1)S(1)}, f32[3,1,2048]{2,1,0:T(1,128)S(1)}) custom-call(s32[4]{0:T(128)S(1)} %get-tuple-element.235.lo_ref, s32[4]{0:T(128)S(1)} %get-tuple-element.234.hi_ref, s32[1]{0:T(128)} %bitcast.29.place_ref, ...), custom_call_target="tpu_custom_call" | custom-call | flops 10066329600 | bytes 12582912 | tf_op jit(solution)/shard_map/attend/pallas_call | solution.py:373
  128.4 1.5 copy-done.44
  134.7 1.9 collective-permute-done.20.arr_ref
  138.2 1.8 collective-permute-start.23
  141.1 22.2 %feed.2 = (f32[512,768]{1,0:T(8,128)S(1)}, bf16[512,768]{1,0:T(8,128)(2,1)S(1)}, f32[512,768]{1,0:T(8,128)S(1)}, bf16[512,768]{1,0:T(8,128)(2,1)S(1)}, f32[768,3072]{1,0:T(8,128)}) custom-call(bf16[512,768]{1,0:T(8,128)(2,1)S(1)} %get-tuple-element.119.n0, bf16[512,768]{1,0:T(8,128)(2,1)S(1)} %collective-permute-done.21.n1, ...), custom_call_target="tpu_custom_call" | custom-call | flops 14495514624 | bytes 14155776 | tf_op jit(solution)/shard_map/feed/pallas_call | solution.py:551
  166.8 2.6 after_feed.2
  171.7 2.0 out_back.2
  175.7 1.6 collective-permute-start.30
  177.6 22.2 %feed.3 = (f32[512,768]{1,0:T(8,128)S(1)}, bf16[512,768]{1,0:T(8,128)(2,1)S(1)}, f32[512,768]{1,0:T(8,128)S(1)}, bf16[512,768]{1,0:T(8,128)(2,1)S(1)}, bf16[768,3072]{1,0:T(8,128)(2,1)}) custom-call(bf16[512,768]{1,0:T(8,128)(2,1)S(1)} %get-tuple-element.138.n0, bf16[512,768]{1,0:T(8,128)(2,1)S(1)} %collective-permute-done.28.n1, ...), custom_call_target="tpu_custom_call" | custom-call | flops 14495514624 | bytes 14155776 | tf_op jit(solution)/shard_map/feed/pallas_call | solution.py:551
  200.4 1.8 collective-permute-done.31.b1_ref
  203.3 2.6 after_feed.3
  208.1 1.4 collective-permute-done.33.g1_ref
  210.4 5.6 %out_back.3 = (bf16[192,1024]{1,0:T(8,128)(2,1)}, bf16[192,1024]{1,0:T(8,128)(2,1)}, f32[768,192]{1,0:T(8,128)}, bf16[768,192]{1,0:T(8,128)(2,1)}) custom-call(s32[1]{0:T(128)} %bitcast.29.place_ref, bf16[512,768]{1,0:T(8,128)(2,1)} %copy-done.20, bf16[512,768]{1,0:T(8,128)(2,1)} %copy-done.66, bf16[192,1024]{1,0:T(8,128)(2,1)} %copy-done.32, ...), custom_call_target="tpu_custom_call" | custom-call | flops 2415919104 | bytes 3145728 | tf_op jit(solution)/shard_map/out_back/pallas_call | solution.py:667
  216.0 1.8 collective-permute-start.36
  218.0 36.3 %attend_back.2 = (f32[2,512,768]{2,1,0:T(8,128)}, bf16[2,512,768]{2,1,0:T(8,128)(2,1)}, bf16[576,2048]{1,0:T(8,128)(2,1)}, f32[2,768]{1,0:T(2,128)S(1)}) custom-call(s32[8]{0:T(128)S(1)} %get-tuple-element.276.lo_ref, s32[8]{0:T(128)S(1)} %get-tuple-element.275.hi_ref, s32[1]{0:T(128)} %bitcast.29.place_ref, bf16[576,2048]{1,0:T(8,128)(2,1)} %copy-done.45, ...), custom_call_target="tpu_custom_call" | custom-call | flops 45298483200 | bytes 12582912 | tf_op jit(solution)/shard_map/attend_back/pallas_call | solution.py:429
  255.3 13.3 %collective-permute-start.38 = (bf16[2,2,96,192]{3,2,1,0:T(8,128)(2,1)}, bf16[2,2,96,192]{3,2,1,0:T(8,128)(2,1)}, u32[]{:S(2)}, u32[]{:S(2)}) collective-permute-start(bf16[2,2,96,192]{3,2,1,0:T(8,128)(2,1)} %fusion.7), channel_id=1, source_target_pairs={{0,4},{4,0},{8,12},{12,8},{16,20},{20,16},{24,28},{28,24},{1,5},{5... | collective-permute-start | bytes 442376 | tf_op jit(solution)/shard_map/ppermute | solution.py:41
  268.6 6.7 %project_grad.2.rest_0_ = f32[768,576]{1,0:T(8,128)} custom-call(bf16[2048,768]{1,0:T(8,128)(2,1)} %get-tuple-element.168.normed_ref, bf16[576,2048]{1,0:T(8,128)(2,1)} %get-tuple-element.169.back_ref), custom_call_target="tpu_custom_call" | custom-call | flops 36238786560 | bytes 6291456 | tf_op jit(solution)/shard_map/project_grad/pallas_call | solution.py:344
  275.4 2.3 fusion
  277.7 1.7 collective-permute-start.37
  279.4 44.8 %attend_back.3 = (f32[2,512,768]{2,1,0:T(8,128)}, bf16[2,512,768]{2,1,0:T(8,128)(2,1)}, bf16[576,2048]{1,0:T(8,128)(2,1)}, f32[2,768]{1,0:T(2,128)S(1)}) custom-call(s32[8]{0:T(128)S(1)} %get-tuple-element.274.lo_ref, s32[8]{0:T(128)S(1)} %get-tuple-element.273.hi_ref, s32[1]{0:T(128)} %bitcast.29.place_ref, bf16[576,2048]{1,0:T(8,128)(2,1)} %copy-done.44, ...), custom_call_target="tpu_custom_call" | custom-call | flops 45298483200 | bytes 12582912 | tf_op jit(solution)/shard_map/attend_back/pallas_call | solution.py:429
  325.8 7.4 %project_grad.3 = f32[768,576]{1,0:T(8,128)} custom-call(bf16[2048,768]{1,0:T(8,128)(2,1)} %get-tuple-element.184.normed_ref, bf16[576,2048]{1,0:T(8,128)(2,1)} %get-tuple-element.185.back_ref, f32[768,576]{1,0:T(8,128)} %project_grad.2.rest_0_), custom_call_target="tpu_custom_call" | custom-call | flops 36238786560 | bytes 6291456 | tf_op jit(solution)/shard_map/project_grad/pallas_call | solution.py:344
  333.2 2.2 fusion.1
  338.0 1.6 collective-permute-start.40
  340.9 4.3 %collective-permute-start.45 = (f32[2,2,4608]{2,1,0:T(2,128)S(1)}, f32[2,2,4608]{2,1,0:T(2,128)S(1)}, u32[]{:S(2)}, u32[]{:S(2)}) collective-permute-start(f32[2,2,4608]{2,1,0:T(2,128)S(1)} %get-tuple-element.256), channel_id=1, source_target_pairs={{0,8},{4,12},{8,0},{12,4},{16,24},{20,28},{24,16},{28,20},{1,9},{5... | collective-permute-start | bytes 221192 | tf_op jit(solution)/shard_map/ppermute | solution.py:41
  345.2 2.4 fusion.3
  348.6 4.5 %finish.2.rest_0_ = f32[2,512,768]{2,1,0:T(8,128)} custom-call(f32[2,4608]{1,0:T(2,128)} %copy-done.2, bf16[2,512,768]{2,1,0:T(8,128)(2,1)} %tok_ref.11, f32[2,512,768]{2,1,0:T(8,128)} %get-tuple-element.166.keep_ref, bf16[2,512,768]{2,1,0:T(8,128)(2,1)} %copy-done.49, bf16[512,768]{1,0:T(8,128)(2,1)} %copy-done.52, f32[512,768]{1,0:T(8,128)} %copy-done.3), custom_call_target="tpu_custom_call" | custom-call | flops 15728640 | bytes 12582912 | tf_op jit(solution)/shard_map/finish/pallas_call | solution.py:751
  356.1 1.9 collective-permute-done.40.crossed_ref
  361.7 4.2 %finish.3 = f32[2,512,768]{2,1,0:T(8,128)} custom-call(f32[2,4608]{1,0:T(2,128)} %copy-done.2, bf16[2,512,768]{2,1,0:T(8,128)(2,1)} %tok_ref.11, f32[2,512,768]{2,1,0:T(8,128)} %get-tuple-element.180.keep_ref, bf16[2,512,768]{2,1,0:T(8,128)(2,1)} %collective-permute-done.39.arr_ref, ...), custom_call_target="tpu_custom_call", output_to_operand_aliasing={{}: (6, {})} | custom-call | flops 15728640 | bytes 12582912 | tf_op jit(solution)/shard_map/finish/pallas_call | solution.py:751
  368.3 1.7 collective-permute-start.50
  370.0 4.7 %collective-permute-done.49 = bf16[96,768]{1,0:T(8,128)(2,1)S(1)} collective-permute-done((bf16[96,768]{1,0:T(8,128)(2,1)S(1)}, bf16[96,768]{1,0:T(8,128)(2,1)S(1)}, u32[]{:S(2)}, u32[]{:S(2)}) %collective-permute-start.49) | collective-permute-done | bytes 147488 | tf_op jit(solution)/shard_map/ppermute | solution.py:41
  (313 shorter events, 55.7 us)
Async XLA Ops:
  7.2 123.4 %all-gather.3.cloned.1.call-start = ((), (), s32[]{:S(2)}) async-start(), calls=%async_computation.2 | async-start | bytes 5849088 | tf_op jit(solution)/shard_map/all_gather | solution.py:863
  8.6 34.5 %collective-permute-start.5 = (bf16[512,768]{1,0:T(8,128)(2,1)S(1)}, bf16[512,768]{1,0:T(8,128)(2,1)S(1)}, u32[]{:S(2)}, u32[]{:S(2)}) collective-permute-start(bf16[512,768]{1,0:T(8,128)(2,1)S(1)} %slice_bitcast_fusion.3.t0), channel_id=1, source_target_pairs={{0,2},{1,3},{2,0},{3,1},{4,6},{5,7},{6,4},{7,5},{8,10},{9,11},{10,... | collective-permute-start | bytes 2359304 | tf_op jit(solution)/shard_map/ppermute | solution.py:33
  11.6 56.8 %collective-permute-start.17 = (bf16[512,768]{1,0:T(8,128)(2,1)S(1)}, bf16[512,768]{1,0:T(8,128)(2,1)}, u32[]{:S(2)}, u32[]{:S(2)}) collective-permute-start(bf16[512,768]{1,0:T(8,128)(2,1)S(1)} %slice_bitcast_fusion.3.t0), channel_id=1, source_target_pairs={{0,1},{1,0},{2,3},{3,2},{4,5},{5,4},{6,7},{7,6},{8,9},{9,8},{10,11... | collective-permute-start | bytes 2359304 | tf_op jit(solution)/shard_map/ppermute | solution.py:37
  11.6 5.5 %collective-permute-start = (f32[2]{0:T(128)S(1)}, f32[2]{0:T(128)S(1)}, u32[]{:S(2)}, u32[]{:S(2)}) collective-permute-start(f32[2]{0:T(128)S(1)} %get-tuple-element.272), channel_id=1, source_target_pairs={{0,4},{4,0},{8,12},{12,8},{16,20},{20,16},{24,28},{28,24},{1,5},{5... | collective-permute-start | bytes 32 | tf_op jit(solution)/shard_map/ppermute | solution.py:41
  13.2 8.9 %collective-permute-start.1 = (bf16[96,576]{1,0:T(8,128)(2,1)S(1)}, bf16[96,576]{1,0:T(8,128)(2,1)S(1)}, u32[]{:S(2)}, u32[]{:S(2)}) collective-permute-start(bf16[96,576]{1,0:T(8,128)(2,1)S(1)} %copy-done.57), channel_id=1, source_target_pairs={{0,16},{4,20},{8,24},{12,28},{16,0},{20,4},{24,8},{28,12},{1,17},{... | collective-permute-start | bytes 331784 | tf_op jit(solution)/shard_map/ppermute | solution.py:41
  22.2 5.4 %collective-permute-start.4 = (f32[2,2]{1,0:T(2,128)S(1)}, f32[2,2]{1,0:T(2,128)S(1)}, u32[]{:S(2)}, u32[]{:S(2)}) collective-permute-start(f32[2,2]{1,0:T(2,128)S(1)} %pad_maximum_fusion.12), channel_id=1, source_target_pairs={{0,24},{4,28},{8,16},{12,20},{16,8},{20,12},{24,0},{28,4},{1,25},{... | collective-permute-start | bytes 56 | tf_op jit(solution)/shard_map/ppermute | solution.py:41
  25.8 4.5 %collective-permute-start.3 = (f32[2,2]{1,0:T(2,128)S(1)}, f32[2,2]{1,0:T(2,128)S(1)}, u32[]{:S(2)}, u32[]{:S(2)}) collective-permute-start(f32[2,2]{1,0:T(2,128)S(1)} %pad_maximum_fusion.12), channel_id=1, source_target_pairs={{0,16},{4,20},{8,24},{12,28},{16,0},{20,4},{24,8},{28,12},{1,17},{... | collective-permute-start | bytes 56 | tf_op jit(solution)/shard_map/ppermute | solution.py:41
  25.8 4.5 %collective-permute-start.2 = (f32[2,2]{1,0:T(2,128)S(1)}, f32[2,2]{1,0:T(2,128)S(1)}, u32[]{:S(2)}, u32[]{:S(2)}) collective-permute-start(f32[2,2]{1,0:T(2,128)S(1)} %pad_maximum_fusion.12), channel_id=1, source_target_pairs={{0,8},{4,12},{8,0},{12,4},{16,24},{20,28},{24,16},{28,20},{1,9},{5... | collective-permute-start | bytes 56 | tf_op jit(solution)/shard_map/ppermute | solution.py:41
  30.5 336.6 %reduce-scatter.2.cloned.1.call-start = ((), (), s32[]{:S(2)}) async-start(), calls=%async_computation.1 | async-start | bytes 5308416 | tf_op jit(solution)/shard_map/reduce_scatter | solution.py:954
  34.0 8.9 %collective-permute-start.6 = (bf16[2,96,576]{2,1,0:T(8,128)(2,1)S(1)}, bf16[2,96,576]{2,1,0:T(8,128)(2,1)S(1)}, u32[]{:S(2)}, u32[]{:S(2)}) collective-permute-start(bf16[2,96,576]{2,1,0:T(8,128)(2,1)S(1)} %pad_maximum_fusion.6), channel_id=1, source_target_pairs={{0,8},{4,12},{8,0},{12,4},{16,24},{20,28},{24,16},{28,20},{1,9},{5... | collective-permute-start | bytes 663560 | tf_op jit(solution)/shard_map/ppermute | solution.py:41
  46.9 6.4 %collective-permute-start.7 = (f32[2,2,2,4608]{3,2,1,0:T(2,128)S(1)}, f32[2,2,2,4608]{3,2,1,0:T(2,128)S(1)}, u32[]{:S(2)}, u32[]{:S(2)}) collective-permute-start(f32[2,2,2,4608]{3,2,1,0:T(2,128)S(1)} %slice_bitcast_fusion.6), channel_id=1, source_target_pairs={{0,4},{4,0},{8,12},{12,8},{16,20},{20,16},{24,28},{28,24},{1,5},{5... | collective-permute-start | bytes 442376 | tf_op jit(solution)/shard_map/ppermute | solution.py:41
  47.4 11.7 %collective-permute-start.13 = (bf16[2,2,96,576]{3,2,0,1:T(8,128)(2,1)S(1)}, bf16[2,2,96,576]{3,2,0,1:T(8,128)(2,1)S(1)}, u32[]{:S(2)}, u32[]{:S(2)}) collective-permute-start(bf16[2,2,96,576]{3,2,0,1:T(8,128)(2,1)S(1)} %pad_maximum_fusion.2), channel_id=1, source_target_pairs={{0,4},{4,0},{8,12},{12,8},{16,20},{20,16},{24,28},{28,24},{1,5},{5... | collective-permute-start | bytes 1327112 | tf_op jit(solution)/shard_map/ppermute | solution.py:41
  53.3 6.0 %collective-permute-start.10 = (f32[2,4608]{1,0:T(2,128)S(1)}, f32[2,4608]{1,0:T(2,128)S(1)}, u32[]{:S(2)}, u32[]{:S(2)}) collective-permute-start(f32[2,4608]{1,0:T(2,128)S(1)} %get-tuple-element.253), channel_id=1, source_target_pairs={{0,24},{4,28},{8,16},{12,20},{16,8},{20,12},{24,0},{28,4},{1,25},{... | collective-permute-start | bytes 110600 | tf_op jit(solution)/shard_map/ppermute | solution.py:41
  53.4 5.9 %collective-permute-start.8 = (f32[2,4608]{1,0:T(2,128)S(1)}, f32[2,4608]{1,0:T(2,128)S(1)}, u32[]{:S(2)}, u32[]{:S(2)}) collective-permute-start(f32[2,4608]{1,0:T(2,128)S(1)} %get-tuple-element.254), channel_id=1, source_target_pairs={{0,8},{4,12},{8,0},{12,4},{16,24},{20,28},{24,16},{28,20},{1,9},{5... | collective-permute-start | bytes 110600 | tf_op jit(solution)/shard_map/ppermute | solution.py:41
  54.4 7.4 %collective-permute-start.9 = (f32[2,4608]{1,0:T(2,128)S(1)}, f32[2,4608]{1,0:T(2,128)S(1)}, u32[]{:S(2)}, u32[]{:S(2)}) collective-permute-start(f32[2,4608]{1,0:T(2,128)S(1)} %get-tuple-element.252), channel_id=1, source_target_pairs={{0,16},{4,20},{8,24},{12,28},{16,0},{20,4},{24,8},{28,12},{1,17},{... | collective-permute-start | bytes 110600 | tf_op jit(solution)/shard_map/ppermute | solution.py:41
  59.2 2.6 collective-permute-start.11
  61.9 4.8 %collective-permute-start.12 = (f32[2,4608]{1,0:T(2,128)S(1)}, f32[2,4608]{1,0:T(2,128)S(1)}, u32[]{:S(2)}, u32[]{:S(2)}) collective-permute-start(f32[2,4608]{1,0:T(2,128)S(1)} %fusion.10), channel_id=1, source_target_pairs={{0,2},{1,3},{2,0},{3,1},{4,6},{5,7},{6,4},{7,5},{8,10},{9,11},{10,... | collective-permute-start | bytes 110600 | tf_op jit(solution)/shard_map/ppermute | solution.py:33
  68.1 28.9 %collective-permute-start.15 = (bf16[512,768]{1,0:T(8,128)(2,1)S(1)}, bf16[512,768]{1,0:T(8,128)(2,1)S(1)}, u32[]{:S(2)}, u32[]{:S(2)}) collective-permute-start(bf16[512,768]{1,0:T(8,128)(2,1)S(1)} %slice_bitcast_fusion.2.t0), channel_id=1, source_target_pairs={{0,1},{1,0},{2,3},{3,2},{4,5},{5,4},{6,7},{7,6},{8,9},{9,8},{10,11... | collective-permute-start | bytes 2359304 | tf_op jit(solution)/shard_map/ppermute | solution.py:37
  68.3 26.7 %collective-permute-start.16 = (bf16[512,768]{1,0:T(8,128)(2,1)S(1)}, bf16[512,768]{1,0:T(8,128)(2,1)S(1)}, u32[]{:S(2)}, u32[]{:S(2)}) collective-permute-start(bf16[512,768]{1,0:T(8,128)(2,1)S(1)} %slice_bitcast_fusion.2.t0), channel_id=1, source_target_pairs={{0,2},{1,3},{2,0},{3,1},{4,6},{5,7},{6,4},{7,5},{8,10},{9,11},{10,... | collective-permute-start | bytes 2359304 | tf_op jit(solution)/shard_map/ppermute | solution.py:33
  95.0 2.4 collective-permute-start.18
  95.5 34.3 %collective-permute-start.19 = (bf16[192,1024]{1,0:T(8,128)(2,1)S(1)}, bf16[192,1024]{1,0:T(8,128)(2,1)S(1)}, u32[]{:S(2)}, u32[]{:S(2)}) collective-permute-start(bf16[192,1024]{1,0:T(8,128)(2,1)S(1)} %get-tuple-element.114.far_ref), channel_id=1, source_target_pairs={{0,2},{1,3},{2,0},{3,1},{4,6},{5,7},{6,4},{7,5},{8,10},{9,11},{10,... | collective-permute-start | bytes 1179656 | tf_op jit(solution)/shard_map/ppermute | solution.py:33
  134.3 2.4 collective-permute-start.20
  137.6 2.4 collective-permute-start.21
  138.1 3.0 collective-permute-start.22
  138.2 25.1 %collective-permute-start.23 = (bf16[192,1024]{1,0:T(8,128)(2,1)S(1)}, bf16[192,1024]{1,0:T(8,128)(2,1)S(1)}, u32[]{:S(2)}, u32[]{:S(2)}) collective-permute-start(bf16[192,1024]{1,0:T(8,128)(2,1)S(1)} %copy-done.22), channel_id=1, source_target_pairs={{0,2},{1,3},{2,0},{3,1},{4,6},{5,7},{6,4},{7,5},{8,10},{9,11},{10,... | collective-permute-start | bytes 1179656 | tf_op jit(solution)/shard_map/ppermute | solution.py:33
  163.3 3.1 collective-permute-start.25
  163.7 3.0 collective-permute-start.26
  165.9 3.8 collective-permute-start.24
  170.8 6.5 %collective-permute-start.29 = (bf16[512,768]{1,0:T(8,128)(2,1)S(1)}, bf16[512,768]{1,0:T(8,128)(2,1)S(1)}, u32[]{:S(2)}, u32[]{:S(2)}) collective-permute-start(bf16[512,768]{1,0:T(8,128)(2,1)S(1)} %get-tuple-element.139.g0), channel_id=1, source_target_pairs={{0,1},{1,0},{2,3},{3,2},{4,5},{5,4},{6,7},{7,6},{8,9},{9,8},{10,11... | collective-permute-start | bytes 2359304 | tf_op jit(solution)/shard_map/ppermute | solution.py:37
  175.7 24.2 %collective-permute-start.30 = (bf16[192,1024]{1,0:T(8,128)(2,1)S(1)}, bf16[192,1024]{1,0:T(8,128)(2,1)S(1)}, u32[]{:S(2)}, u32[]{:S(2)}) collective-permute-start(bf16[192,1024]{1,0:T(8,128)(2,1)S(1)} %get-tuple-element.137), channel_id=1, source_target_pairs={{0,2},{1,3},{2,0},{3,1},{4,6},{5,7},{6,4},{7,5},{8,10},{9,11},{10,... | collective-permute-start | bytes 1179656 | tf_op jit(solution)/shard_map/ppermute | solution.py:33
  199.9 2.4 collective-permute-start.31
  200.3 3.1 collective-permute-start.32
  216.0 59.4 %collective-permute-start.36 = (bf16[192,1024]{1,0:T(8,128)(2,1)}, bf16[192,1024]{1,0:T(8,128)(2,1)S(1)}, u32[]{:S(2)}, u32[]{:S(2)}) collective-permute-start(bf16[192,1024]{1,0:T(8,128)(2,1)} %get-tuple-element.158), channel_id=1, source_target_pairs={{0,2},{1,3},{2,0},{3,1},{4,6},{5,7},{6,4},{7,5},{8,10},{9,11},{10,... | collective-permute-start | bytes 1179656 | tf_op jit(solution)/shard_map/ppermute | solution.py:33
  217.8 36.6 %collective-permute-start.34 = (bf16[768,192]{1,0:T(8,128)(2,1)}, bf16[768,192]{1,0:T(8,128)(2,1)S(1)}, u32[]{:S(2)}, u32[]{:S(2)}) collective-permute-start(bf16[768,192]{1,0:T(8,128)(2,1)} %get-tuple-element.165), channel_id=1, source_target_pairs={{0,2},{1,3},{2,0},{3,1},{4,6},{5,7},{6,4},{7,5},{8,10},{9,11},{10,... | collective-permute-start | bytes 884744 | tf_op jit(solution)/shard_map/ppermute | solution.py:33
  254.3 21.1 %collective-permute-start.35 = (bf16[2,512,768]{2,1,0:T(8,128)(2,1)}, bf16[2,512,768]{2,1,0:T(8,128)(2,1)S(1)}, u32[]{:S(2)}, u32[]{:S(2)}) collective-permute-start(bf16[2,512,768]{2,1,0:T(8,128)(2,1)} %get-tuple-element.167), channel_id=1, source_target_pairs={{0,1},{1,0},{2,3},{3,2},{4,5},{5,4},{6,7},{7,6},{8,9},{9,8},{10,11... | collective-permute-start | bytes 4718600 | tf_op jit(solution)/shard_map/ppermute | solution.py:37
  255.3 68.9 %collective-permute-start.38 = (bf16[2,2,96,192]{3,2,1,0:T(8,128)(2,1)}, bf16[2,2,96,192]{3,2,1,0:T(8,128)(2,1)}, u32[]{:S(2)}, u32[]{:S(2)}) collective-permute-start(bf16[2,2,96,192]{3,2,1,0:T(8,128)(2,1)} %fusion.7), channel_id=1, source_target_pairs={{0,4},{4,0},{8,12},{12,8},{16,20},{20,16},{24,28},{28,24},{1,5},{5... | collective-permute-start | bytes 442376 | tf_op jit(solution)/shard_map/ppermute | solution.py:41
  277.7 46.5 %collective-permute-start.37 = (bf16[512,768]{1,0:T(8,128)(2,1)S(1)}, bf16[512,768]{1,0:T(8,128)(2,1)S(1)}, u32[]{:S(2)}, u32[]{:S(2)}) collective-permute-start(bf16[512,768]{1,0:T(8,128)(2,1)S(1)} %fusion), channel_id=1, source_target_pairs={{0,2},{1,3},{2,0},{3,1},{4,6},{5,7},{6,4},{7,5},{8,10},{9,11},{10,... | collective-permute-start | bytes 2359304 | tf_op jit(solution)/shard_map/ppermute | solution.py:33
  325.1 8.1 %collective-permute-start.39 = (bf16[2,512,768]{2,1,0:T(8,128)(2,1)}, bf16[2,512,768]{2,1,0:T(8,128)(2,1)}, u32[]{:S(2)}, u32[]{:S(2)}) collective-permute-start(bf16[2,512,768]{2,1,0:T(8,128)(2,1)} %get-tuple-element.181), channel_id=1, source_target_pairs={{0,1},{1,0},{2,3},{3,2},{4,5},{5,4},{6,7},{7,6},{8,9},{9,8},{10,11... | collective-permute-start | bytes 4718600 | tf_op jit(solution)/shard_map/ppermute | solution.py:37
  325.2 8.0 %collective-permute-start.42 = (f32[2,4608]{1,0:T(2,128)S(1)}, f32[2,4608]{1,0:T(2,128)S(1)}, u32[]{:S(2)}, u32[]{:S(2)}) collective-permute-start(f32[2,4608]{1,0:T(2,128)S(1)} %pad_maximum_fusion.8), channel_id=1, source_target_pairs={{0,2},{1,3},{2,0},{3,1},{4,6},{5,7},{6,4},{7,5},{8,10},{9,11},{10,... | collective-permute-start | bytes 110600 | tf_op jit(solution)/shard_map/ppermute | solution.py:33
  336.7 4.0 %collective-permute-start.44 = (f32[2,4608]{1,0:T(2,128)S(1)}, f32[2,4608]{1,0:T(2,128)S(1)}, u32[]{:S(2)}, u32[]{:S(2)}) collective-permute-start(f32[2,4608]{1,0:T(2,128)S(1)} %get-tuple-element.239), channel_id=1, source_target_pairs={{0,4},{4,0},{8,12},{12,8},{16,20},{20,16},{24,28},{28,24},{1,5},{5... | collective-permute-start | bytes 110600 | tf_op jit(solution)/shard_map/ppermute | solution.py:41
  338.0 20.0 %collective-permute-start.40 = (bf16[512,768]{1,0:T(8,128)(2,1)}, bf16[512,768]{1,0:T(8,128)(2,1)}, u32[]{:S(2)}, u32[]{:S(2)}) collective-permute-start(bf16[512,768]{1,0:T(8,128)(2,1)} %fusion.1), channel_id=1, source_target_pairs={{0,2},{1,3},{2,0},{3,1},{4,6},{5,7},{6,4},{7,5},{8,10},{9,11},{10,... | collective-permute-start | bytes 2359304 | tf_op jit(solution)/shard_map/ppermute | solution.py:33
  340.8 12.4 %collective-permute-start.47 = (f32[2,2,4608]{2,1,0:T(2,128)S(1)}, f32[2,2,4608]{2,1,0:T(2,128)S(1)}, u32[]{:S(2)}, u32[]{:S(2)}) collective-permute-start(f32[2,2,4608]{2,1,0:T(2,128)S(1)} %get-tuple-element.256), channel_id=1, source_target_pairs={{0,24},{4,28},{8,16},{12,20},{16,8},{20,12},{24,0},{28,4},{1,25},{... | collective-permute-start | bytes 221192 | tf_op jit(solution)/shard_map/ppermute | solution.py:41
  340.8 12.3 %collective-permute-start.46 = (f32[2,2,4608]{2,1,0:T(2,128)S(1)}, f32[2,2,4608]{2,1,0:T(2,128)S(1)}, u32[]{:S(2)}, u32[]{:S(2)}) collective-permute-start(f32[2,2,4608]{2,1,0:T(2,128)S(1)} %get-tuple-element.256), channel_id=1, source_target_pairs={{0,16},{4,20},{8,24},{12,28},{16,0},{20,4},{24,8},{28,12},{1,17},{... | collective-permute-start | bytes 221192 | tf_op jit(solution)/shard_map/ppermute | solution.py:41
  340.9 12.3 %collective-permute-start.45 = (f32[2,2,4608]{2,1,0:T(2,128)S(1)}, f32[2,2,4608]{2,1,0:T(2,128)S(1)}, u32[]{:S(2)}, u32[]{:S(2)}) collective-permute-start(f32[2,2,4608]{2,1,0:T(2,128)S(1)} %get-tuple-element.256), channel_id=1, source_target_pairs={{0,8},{4,12},{8,0},{12,4},{16,24},{20,28},{24,16},{28,20},{1,9},{5... | collective-permute-start | bytes 221192 | tf_op jit(solution)/shard_map/ppermute | solution.py:41
  347.6 11.5 %collective-permute-start.41 = (bf16[2,2,96,576]{3,2,1,0:T(8,128)(2,1)}, bf16[2,2,96,576]{3,2,1,0:T(8,128)(2,1)S(1)}, u32[]{:S(2)}, u32[]{:S(2)}) collective-permute-start(bf16[2,2,96,576]{3,2,1,0:T(8,128)(2,1)} %fusion.3), channel_id=1, source_target_pairs={{0,4},{4,0},{8,12},{12,8},{16,20},{20,16},{24,28},{28,24},{1,5},{5... | collective-permute-start | bytes 1327112 | tf_op jit(solution)/shard_map/ppermute | solution.py:41
  359.7 7.2 %collective-permute-start.48 = (bf16[2,96,768]{2,1,0:T(8,128)(2,1)S(1)}, bf16[2,96,768]{2,1,0:T(8,128)(2,1)S(1)}, u32[]{:S(2)}, u32[]{:S(2)}) collective-permute-start(bf16[2,96,768]{2,1,0:T(8,128)(2,1)S(1)} %fusion.4), channel_id=1, source_target_pairs={{0,8},{4,12},{8,0},{12,4},{16,24},{20,28},{24,16},{28,20},{1,9},{5... | collective-permute-start | bytes 884744 | tf_op jit(solution)/shard_map/ppermute | solution.py:41
  367.0 7.7 %collective-permute-start.49 = (bf16[96,768]{1,0:T(8,128)(2,1)S(1)}, bf16[96,768]{1,0:T(8,128)(2,1)S(1)}, u32[]{:S(2)}, u32[]{:S(2)}) collective-permute-start(bf16[96,768]{1,0:T(8,128)(2,1)S(1)} %fusion.8), channel_id=1, source_target_pairs={{0,16},{4,20},{8,24},{12,28},{16,0},{20,4},{24,8},{28,12},{1,17},{... | collective-permute-start | bytes 442376 | tf_op jit(solution)/shard_map/ppermute | solution.py:41
  368.3 8.0 %collective-permute-start.50 = (bf16[96,1536]{1,0:T(8,128)(2,1)S(1)}, bf16[96,1536]{1,0:T(8,128)(2,1)S(1)}, u32[]{:S(2)}, u32[]{:S(2)}) collective-permute-start(bf16[96,1536]{1,0:T(8,128)(2,1)S(1)} %broadcast_select_fusion), channel_id=1, source_target_pairs={{0,2},{1,3},{2,0},{3,1},{4,6},{5,7},{6,4},{7,5},{8,10},{9,11},{10,... | collective-permute-start | bytes 884744 | tf_op jit(solution)/shard_map/ppermute | solution.py:33
  (74 other events, 712.7 us)
Sparse Core Ops, SparseCore 0:
  30.6 97.2 all-gather.2
  207.7 102.7 reduce-scatter.1
